TPU v7x, 32 devices: a whole 2x2x4 slice. The times are simulated.
32 devices in a mesh: slab: 8 (over y, x, core), cross: 4 (over z).
Axes of the slice: x: 2, y: 2, z: 4, core: 2. Of those that a mesh axis runs over, the one named last changes fastest.
Arguments:
- positions: float32 [3, 4096], P(None, ('slab', 'cross')), as said below
- velocities: float32 [3, 4096], P(None, ('slab', 'cross')), may hold values from -3 to 3
- inverse_mass: float32 [4096], P(('slab', 'cross')), may hold values from 0.0625 to 1
- species: int32 [4096], P(('slab', 'cross')), may hold values from 0 to 7
- type_table: float32 [8, 128], replicated, may hold values from -5 to 5
- neighbours: int32 [4096, 16], P(('slab', 'cross')), may hold values from 0 to 639, as said below
- slot_count: int32 [4096], P(('slab', 'cross')), may hold values from 0 to 16, as said below
- atom_count: int32 [32], P(('slab', 'cross')), may hold values from 96 to 128
- pair_bins: int32 [4096, 16], P(('slab', 'cross')), may hold values from 0 to 127
- send_list: int32 [16, 8, 32], P('slab', 'cross'), may hold values from 0 to 127, as said below
- target: float32 [128], replicated, may hold values from 0 to 0.5
- encoder: float32 [128, 128], replicated, may hold values from -0.5 to 0.5
- spreader: float32 [128, 256], replicated, may hold values from -0.5 to 0.5
- filters: float32 [20, 256], replicated, may hold values from -1.25 to 1.25
- rotator: float32 [128, 128], replicated, may hold values from -0.5 to 0.5
- reflector: float32 [128, 128], replicated, may hold values from -0.5 to 0.5
- combiner: float32 [256, 128], replicated, may hold values from -0.375 to 0.375
- splitter: float32 [128, 256], replicated, may hold values from -0.5 to 0.5
- readout: float32 [128, 128], replicated, may hold values from -0.5 to 0.5
- collector: float32 [128], replicated, may hold values from -0.5 to 0.5
Outputs:
- next_positions: float32 [3, 4096], P(None, ('slab', 'cross'))
- position_adjoint: float32 [3, 4096], P(None, ('slab', 'cross'))
- encoder_grad: float32 [128, 128], P('cross')
- spreader_grad: float32 [128, 256], P('cross')
- filters_grad: float32 [20, 256], P(None, 'cross')
- rotator_grad: float32 [128, 128], P('cross')
- reflector_grad: float32 [128, 128], P('cross')
- combiner_grad: float32 [256, 128], P('cross')
- splitter_grad: float32 [128, 256], P('cross')
- readout_grad: float32 [128, 128], P('cross')
- collector_grad: float32 [128], P('cross')
Inputs may be any that keep to these rules, and one draw needn't show every extreme that they name: `neighbours`: rows of the device's pool; a live slot never names the atom itself, a dead atom, or a block (p, q) with p and q both in 1..2; live slots come before dead ones. `slot_count`: 0 for atoms at or beyond the device's atom_count. The four blocks send_list[2 s + a, 2 c + b], a and b in 0..1, of device (s, c) list each of its 128 atom rows exactly once. `positions`: A device's atoms lie in its local box of 10 by 10 by 1.6 * 8 Angstrom.
All inputs are finite; a program needn't handle non-finite values.
Results may differ from a plain program's by a relative error of at most 0.0003.
Values sent between devices are 32-bit elements; how exact they have to be, the bound alone decides.
No kernel may reach another device: no remote copies, remote signals or barrier semaphores. Data moves between devices by JAX's collectives and lax.ppermute only.
A program may use at most 128 MiB of HBM per device.

v0:
```python
import functools

import jax
import jax.numpy as jnp
from jax import lax
from jax.experimental import pallas as pl
from jax.experimental.pallas import tpu as pltpu
from jax.sharding import PartitionSpec as P


cutoff = 5.0
soften = 0.25
sigma_two = 0.18
slab_length = 10.0
cell_length = 10.0
time_step = 0.5
highest = lax.Precision.HIGHEST
f32 = jnp.float32
bf16 = jnp.bfloat16
pi = 3.141592653589793
omega = pi / cutoff

NN = ((1,), (0,))
NT = ((1,), (1,))
VM = pl.BlockSpec(memory_space=pltpu.VMEM)
SM = pl.BlockSpec(memory_space=pltpu.SMEM)
HB = pl.BlockSpec(memory_space=pltpu.HBM)


def call(body, outs, *args, specs=None, scratch=(), keep=True):
    return pl.pallas_call(
        body,
        out_shape=[(pltpu.VMEM if keep else jax.ShapeDtypeStruct)(s, d) for s, d in outs],
        in_specs=[VM] * len(args) if specs is None else specs,
        out_specs=[VM] * len(outs),
        scratch_shapes=list(scratch),
        compiler_params=pltpu.CompilerParams(vmem_limit_bytes=16 * 2**20),
    )(*args)


def in_hbm(*arrays):
    return [pltpu.with_memory_space_constraint(x, pltpu.HBM) for x in arrays]


def fetch(sources, targets, semaphores):
    copies = [
        pltpu.make_async_copy(source, target, semaphores.at[i])
        for i, (source, target) in enumerate(zip(sources, targets))
    ]
    for copy in copies:
        copy.start()
    for copy in copies:
        copy.wait()


def split(x):
    high = x.astype(bf16)
    return high, (x - high.astype(f32)).astype(bf16)


def dot1(a, b, dims):
    return lax.dot_general(a, b, (dims, ((), ())), preferred_element_type=f32)


def dot3(a, b, dims=NN):
    return dot1(
        jnp.concatenate([a[0], a[0], a[1]], dims[0][0]), jnp.concatenate([b[0], b[1], b[0]], dims[1][0]), dims
    )


def cat(parts, axis):
    return jnp.concatenate(parts, axis=axis)


def iota(shape, dim):
    return lax.broadcasted_iota(jnp.int32, shape, dim)


def lane_take(row, index):
    return jnp.take_along_axis(jnp.broadcast_to(row, index.shape), index, axis=1)


def own_lanes(group, lanes):
    quarter = lanes // 4
    start = 2 * quarter * (1 - group // 2) + quarter * (1 - group % 2)
    return start, quarter


def pool_offsets(group, lanes):
    place = iota((1, lanes), 1)
    up, right = group // 2, group % 2
    half, quarter = lanes // 2, lanes // 4
    first = (place >= half) if up else (place < half)
    second_bit = place % half >= quarter
    second = second_bit if right else jnp.logical_not(second_bit)
    sign_u, sign_r = 2.0 * up - 1.0, 2.0 * right - 1.0
    return (
        jnp.where(first, sign_u * slab_length, 0.0).astype(f32),
        jnp.where(second, sign_r * cell_length, 0.0).astype(f32),
        None,
    )


def from_pool(rows, code, lanes):
    group = code // lanes
    lane = code % lanes
    out = lane_take(rows[0], lane)
    for j in range(1, 4):
        out = jnp.where(group == j, lane_take(rows[j], lane), out)
    return out


def pool_deltas(pool_rows, own_rows, code, lanes, depth):
    deltas = []
    for c in range(3):
        d = from_pool([pool_rows(j, c) for j in range(4)], code, lanes) - own_rows(c)
        if c == 2:
            d = d - depth * jnp.floor(d / depth + 0.5)
        deltas.append(d)
    radius = jnp.sqrt(deltas[0] * deltas[0] + deltas[1] * deltas[1] + deltas[2] * deltas[2] + soften)
    return deltas, radius


def one_hot_rows(index, slots, count):
    lanes = index.shape[1]
    place = iota((count, lanes), 0)
    return cat(
        [(place == index[k : k + 1, :]).astype(f32).astype(bf16) for k in range(slots)], 1
    )


def scatter_lanes(values, index, scratch, count):
    shape = index.shape
    slots = shape[0]
    for row in range(16):
        value = values[row] if row < len(values) else None
        if value is None:
            value = jnp.zeros(shape, f32)
        scratch[pl.ds(row, slots, stride=16), :] = value
    highs, mids, lows = [], [], []
    for k in range(slots):
        x = scratch[16 * k : 16 * k + 16, :]
        high = x.astype(bf16)
        rest = x - high.astype(f32)
        mid = rest.astype(bf16)
        highs.append(high)
        mids.append(mid)
        lows.append((rest - mid.astype(f32)).astype(bf16))
    left = cat([cat(highs, 1), cat(mids, 1), cat(lows, 1)], 0)
    sums = dot1(left, one_hot_rows(index, slots, count), NT)
    return sums[0:16] + (sums[16:32] + sums[32:48])


def pool_partials(deltas_bar, code, send_index, outs, scratch, lanes):
    group = code // lanes
    values = []
    for j in range(4):
        for c in range(3):
            values.append(jnp.where(group == j, deltas_bar[c], 0.0))
        values.append(None)
    sums = scatter_lanes(values, code % lanes, scratch, lanes)
    centres = [-jnp.sum(d, axis=0, keepdims=True) for d in deltas_bar]
    place = iota((1, lanes), 1)
    for j in range(4):
        start, width = own_lanes(j, lanes)
        own = jnp.logical_and(place >= start, place < start + width)
        out_ref = outs[j // 2]
        out_ref[j % 2, :, :] = jnp.zeros((8, lanes), f32)
        for c in range(3):
            mine = lane_take(jnp.broadcast_to(centres[c], (8, lanes)), jnp.broadcast_to(send_index(j), (8, lanes)))
            out_ref[j % 2, c : c + 1, :] = sums[4 * j + c : 4 * j + c + 1, :] + jnp.where(
                own, mine[0:1, :], 0.0
            )


def offer_body(
    pos, vel, mass, species, send_list, low, high, own_out, send_out,
    pos_v, vel_v, mass_v, species_v, list_v, semaphores,
):
    fetch((pos, vel, mass, species, send_list), (pos_v, vel_v, mass_v, species_v, list_v), semaphores)
    lanes = pos.shape[1]
    own_out[0:3, :] = pos_v[...]
    own_out[3:6, :] = vel_v[...]
    own_out[6:7, :] = mass_v[...]
    own_out[7:8, :] = species_v[...].astype(f32)
    own_rows = own_out[...]
    place = iota((8, lanes), 1)
    send_out[...] = jnp.zeros((8, lanes), jnp.int32)
    for j in range(4):
        start, width = own_lanes(j, lanes)
        pieces = [list_v[j // 2, j % 2 : j % 2 + 1, :]]
        if start:
            pieces = [jnp.zeros((1, start), jnp.int32)] + pieces
        if start + width < lanes:
            pieces = pieces + [jnp.zeros((1, lanes - start - width), jnp.int32)]
        row = cat(pieces, 1)
        send_out[j : j + 1, :] = row
        own = jnp.logical_and(place >= start, place < start + width)
        taken = jnp.take_along_axis(own_rows, jnp.broadcast_to(row, (8, lanes)), axis=1)
        out = (low, high)[j // 2]
        out[j % 2, :, :] = jnp.where(own, taken, 0.0)


def turn_body(low, high, from_down, from_up, left, right):
    for u, (mine, other) in enumerate(((low, from_down), (high, from_up))):
        left[u, :, :] = mine[0] + other[0]
        right[u, :, :] = mine[1] + other[1]


def whole(pieces, j):
    right = j % 2
    return pieces[right][j // 2] + pieces[2 + right][j // 2]


class Rows:
    def __init__(self, sizes):
        self.at = {}
        self.total = 0
        for name, size in sizes:
            self.at[name] = (self.total, size)
            self.total += size

    def get(self, ref, name):
        start, size = self.at[name]
        return ref[start : start + size, :]

    def put(self, ref, name, value):
        start, size = self.at[name]
        ref[start : start + size, :] = value


STRIDE = 32
USED = 24


def narrow_rows(feat):
    return Rows((("RQT", 2 * feat), ("C", 2 * feat), ("ST", 2 * feat), ("RT", feat), ("R", feat)))


def wide_rows(feat, types):
    return Rows((("BT", 2 * feat), ("B", STRIDE * types), ("RQ", feat), ("CT", feat), ("S", feat)))


def weights_body(
    table_h, encoder_h, spreader_h, filters_h, rotator_h, reflector_h, combiner_h, splitter_h, readout_h,
    collector_h, col_out, nh, nl, wh, wl, phi_out, slope_out, hidden_t, table_t, filt_out, spreader,
    table, encoder, filters, rotator, reflector, combiner, splitter, readout, collector, semaphores,
):
    fetch(
        (table_h, encoder_h, spreader_h, filters_h, rotator_h, reflector_h, combiner_h, splitter_h, readout_h,
         collector_h),
        (table, encoder, spreader, filters, rotator, reflector, combiner, splitter, readout, collector),
        semaphores,
    )
    types, feat = table.shape
    lanes = hidden_t.shape[1]
    basis = filters.shape[0]
    pre = jnp.dot(table[...], encoder[...], precision=highest, preferred_element_type=f32)
    gate = lax.logistic(pre)
    hidden = pre * gate
    phi = jnp.dot(hidden, spreader[...], precision=highest, preferred_element_type=f32)
    phi_out[...] = phi
    slope_out[...] = gate * (1.0 + pre * (1.0 - gate))
    rest = [jnp.zeros((lanes - types, feat), f32)]
    hidden_t[...] = jnp.transpose(cat([hidden] + rest, 0))
    table_t[...] = jnp.transpose(cat([table[...]] + rest, 0))
    filt_out[...] = jnp.zeros(filt_out.shape, f32)
    filt_out[0:basis, :] = filters[...]
    filt = filt_out[...]
    col_out[...] = jnp.transpose(jnp.broadcast_to(collector[...], (lanes, feat)))
    narrow = narrow_rows(feat)
    wide = wide_rows(feat, types)

    def put(rows, high_ref, low_ref, name, value, row=0, col=0):
        high, low = split(value)
        start = rows.at[name][0] + row
        high_ref[start : start + value.shape[0], col : col + value.shape[1]] = high
        low_ref[start : start + value.shape[0], col : col + value.shape[1]] = low

    per_half = feat // STRIDE
    for half in range(2):
        cols = slice(half * feat, (half + 1) * feat)
        for chunk in range(types // per_half):
            block = cat(
                [
                    filt[:, cols] * phi[t : t + 1, cols]
                    for t in range(chunk * per_half, (chunk + 1) * per_half)
                ],
                0,
            )
            put(wide, wh, wl, "B", block, chunk * feat, half * feat)
            put(wide, wh, wl, "BT", jnp.transpose(block), half * feat, chunk * feat)
    put(wide, wh, wl, "RQ", rotator[...], 0, 0)
    put(wide, wh, wl, "RQ", reflector[...], 0, feat)
    put(narrow, nh, nl, "RQT", jnp.transpose(rotator[...]), 0)
    put(narrow, nh, nl, "RQT", jnp.transpose(reflector[...]), feat)
    put(narrow, nh, nl, "C", combiner[...])
    put(wide, wh, wl, "CT", jnp.transpose(combiner[0:feat, :]), 0, 0)
    put(wide, wh, wl, "CT", jnp.transpose(combiner[feat : 2 * feat, :]), 0, feat)
    put(wide, wh, wl, "S", splitter[...])
    put(narrow, nh, nl, "ST", jnp.transpose(splitter[:, 0:feat]), 0)
    put(narrow, nh, nl, "ST", jnp.transpose(splitter[:, feat : 2 * feat]), feat)
    put(narrow, nh, nl, "R", readout[...])
    put(narrow, nh, nl, "RT", jnp.transpose(readout[...]))


def index_body(
    near_h, count_h, bins_h, target_h, atom_count, send, own_rows, table_t,
    index, masks, feat_out, bins, target, near, slot_count, semaphores,
):
    fetch((near_h, count_h, bins_h, target_h), (near, slot_count, bins, target), semaphores)
    species = own_rows[7:8, :].astype(jnp.int32)
    slots, lanes = near.shape
    quarter = lanes // 4
    lane_row = iota((16, lanes), 1).astype(f32)
    row_id = iota((16, lanes), 0)
    lefts, rights = [], []
    place = iota((lanes, lanes), 1)
    for j in range(4):
        start, width = own_lanes(j, lanes)
        own = jnp.logical_and(place >= start, place < start + width)
        same = jnp.logical_and(own, iota((lanes, lanes), 0) == send[j : j + 1, :])
        rights.append(same.astype(f32).astype(bf16))
        lefts.append(
            jnp.where(row_id == 0, lane_row, jnp.where(row_id == 1, float(j), 0.0)).astype(bf16)
        )
    found = dot1(cat(lefts, 1), cat(rights, 1), NT)
    inverse = (found[0:1, :] + lanes * found[1:2, :] + 0.5).astype(jnp.int32)
    near_v = near[...]
    ghost = near_v - lanes
    block = ghost // quarter
    p, q, g = block // 4, block % 4, ghost % quarter
    ghost_code = (2 * (p // 2) + q // 2) * lanes + 2 * quarter * (p % 2) + quarter * (q % 2) + g
    own_code = lane_take(inverse, jnp.minimum(near_v, lanes - 1))
    index[...] = jnp.zeros(index.shape, jnp.int32)
    index[0:slots, :] = jnp.where(near_v < lanes, own_code, ghost_code)
    index[slots : slots + 4, :] = send[0:4, :]
    index[slots + 4 : slots + 5, :] = inverse
    masks[...] = jnp.zeros(masks.shape, f32)
    masks[0:slots, :] = (iota((slots, lanes), 0) < slot_count[...]).astype(f32)
    masks[slots : slots + 1, :] = (iota((1, lanes), 1) < atom_count[0]).astype(f32)
    feat_out[...] = jnp.take_along_axis(table_t[...], jnp.broadcast_to(species, table_t.shape), axis=1)


def saved_rows(feat, types, slots):
    k = STRIDE * types
    pair = ("e", "e1", "e2", "ir", "u0", "u1", "u2", "t")
    sizes = [("A%d" % q, k) for q in range(4)]
    sizes += [("%s%d" % (n, c), feat) for n in ("v", "vb") for c in range(3)]
    sizes += [("%s%d" % (n, c), 2 * feat) for n in ("uw", "uwb") for c in range(3)]
    sizes += [("joined", 2 * feat), ("ab", 2 * feat)]
    sizes += [
        (n, feat)
        for n in ("z", "dz", "d2z", "a2", "q", "n", "s2", "yb", "yc", "ldy", "s2b", "zb", "hb", "qb", "nbn", "s1b")
    ]
    sizes += [("sin", slots * USED), ("cos", slots * USED), ("mask", 8 * slots * types)]
    sizes += [(n, slots) for n in pair]
    sizes += [("%s%d" % (n, q), slots) for n in ("sa", "sb", "sd") for q in range(4)]
    return Rows(sizes)


def multiples(c1, s1, sin_ref, cos_ref, slots):
    lanes = c1.shape[1]
    powers = [(c1, s1)]
    for _ in range(4):
        c, s = powers[-1]
        powers.append((c * c - s * s, 2.0 * c * s))
    sub = iota((8, lanes), 0)
    bits = [(sub // 2**b) % 2 == 1 for b in range(3)]
    order = sub.astype(f32) + 1.0

    def times(x, y):
        return x[0] * y[0] - x[1] * y[1], x[0] * y[1] + x[1] * y[0]

    for k in range(slots):
        rows = [
            tuple(jnp.broadcast_to(part[k : k + 1, :], (8, lanes)) for part in power)
            for power in powers
        ]
        z = rows[0]
        for b in range(3):
            step = (jnp.where(bits[b], rows[b][0], 1.0), jnp.where(bits[b], rows[b][1], 0.0))
            z = times(z, step)
        for v in range(3):
            if v == 1:
                zv = times(z, rows[3])
            elif v == 2:
                zv = times(z, rows[4])
            else:
                zv = z
            start = k * USED + 8 * v
            sin_ref[start : start + 8, :] = zv[1]
            cos_ref[start : start + 8, :] = zv[0] * ((order + 8.0 * v) * omega)


def type_masks(kinds, types, put):
    slots, lanes = kinds.shape
    for k in range(slots):
        kind = jnp.broadcast_to(kinds[k : k + 1, :], (8, lanes))
        for t in range(types):
            put(k * types + t, jnp.where(kind == t, 1.0, 0.0))


def choose(options, bits):
    for bit in bits:
        options = [
            jnp.where(bit, options[i + 1], options[i]) if i + 1 < len(options) else options[i]
            for i in range(0, len(options), 2)
        ]
    return options[0]


def slot_sums(read_sin, read_cos, sin_coef, cos_coef, read_mask, slots, types, put):
    lanes = sin_coef[0].shape[1]
    tiles = USED // 8
    for q in range(4):
        sums = [[None] * tiles for _ in range(types)]
        for k in range(slots):
            value = read_sin(k) * sin_coef[q][k : k + 1, :]
            if cos_coef is not None:
                value = value + read_cos(k) * cos_coef[q][k : k + 1, :]
            for t in range(types):
                mask = read_mask(k * types + t)
                for v in range(tiles):
                    part = value[8 * v : 8 * v + 8] * mask
                    sums[t][v] = part if sums[t][v] is None else sums[t][v] + part
        rest = jnp.zeros((STRIDE - USED, lanes), f32)
        put(q, cat([x for t in range(types) for x in sums[t] + [rest]], 0))


def slot_reads(values, kinds, read_sin, read_cos, slots, types, put, with_square):
    lanes = kinds.shape[1]
    tiles = USED // 8
    whole_kinds = (kinds + 0.5).astype(jnp.int32)
    kind_bits = [((whole_kinds // 2**b) % 2).astype(f32) for b in range((types - 1).bit_length())]
    square = [((iota((8, lanes), 0).astype(f32) + (8.0 * v + 1.0)) * omega) ** 2 for v in range(tiles)]
    for q in range(4):
        value = values(q)
        tables = [
            [value[STRIDE * t + 8 * v : STRIDE * t + 8 * v + 8] for v in range(tiles)] for t in range(types)
        ]
        for k in range(slots):
            bits = [jnp.broadcast_to(part[k : k + 1, :], (8, lanes)) > 0.5 for part in kind_bits]
            picked = [choose([table[v] for table in tables], bits) for v in range(tiles)]
            sines, cosines = read_sin(k), read_cos(k)
            with_sin = [sines[8 * v : 8 * v + 8] * picked[v] for v in range(tiles)]
            put("sa", q, k, jnp.sum(sum(with_sin), axis=0, keepdims=True))
            with_cos = [cosines[8 * v : 8 * v + 8] * picked[v] for v in range(tiles)]
            put("sb", q, k, jnp.sum(sum(with_cos), axis=0, keepdims=True))
            if with_square:
                with_sin = [with_sin[v] * square[v] for v in range(tiles)]
                put("sd", q, k, jnp.sum(sum(with_sin), axis=0, keepdims=True))


def triple(rows, ref, name):
    return cat([rows.get(ref, "%s%d" % (name, c)) for c in range(3)], 1)


def thirds(value):
    n = value.shape[1] // 3
    return [value[:, c * n : (c + 1) * n] for c in range(3)]


def force_body(
    types, depth, left, right, from_left, from_right, own_rows, index, masks, features, colmat, nh, nl, wh, wl,
    low, high, pool, save, scratch,
):
    lanes = own_rows.shape[1]
    for j in range(4):
        pool[j, :, :] = whole((left, right, from_left, from_right), j)
    slots = index.shape[0] - 8
    feat = features.shape[0]
    rows = saved_rows(feat, types, slots)
    narrow = narrow_rows(feat)
    wide = wide_rows(feat, types)
    code = index[0:slots, :]
    mask = masks[0:slots, :]
    live = masks[slots : slots + 1, :]

    def coords(j, c):
        shift = pool_offsets(j, lanes)[c]
        row = pool[j, c : c + 1, :]
        return row if shift is None else row + shift

    deltas, radius = pool_deltas(coords, lambda c: own_rows[c : c + 1, :], code, lanes, depth)
    kinds = from_pool([pool[j, 7:8, :] for j in range(4)], code, lanes)
    inside = jnp.where(radius < cutoff, mask, 0.0)
    theta = omega * jnp.minimum(radius, cutoff)
    c1, s1 = jnp.cos(theta), jnp.sin(theta)
    ir = 1.0 / radius
    env = 0.5 * (c1 + 1.0) * inside
    e = env * ir
    e1 = ((-0.5 * omega) * s1 * inside - e) * ir
    e2 = ((-0.5 * omega * omega) * c1 * inside - 2.0 * e1) * ir
    unit = [d * ir for d in deltas]
    for name, value in (("e", e), ("e1", e1), ("e2", e2), ("ir", ir), ("t", kinds)):
        rows.put(save, name, value)
    for c in range(3):
        rows.put(save, "u%d" % c, unit[c])
    sin_at, cos_at = rows.at["sin"][0], rows.at["cos"][0]
    multiples(c1, s1, save.at[sin_at : sin_at + slots * USED, :], save.at[cos_at : cos_at + slots * USED, :], slots)

    def read_sin(k):
        return save[sin_at + k * USED : sin_at + (k + 1) * USED, :]

    def read_cos(k):
        return save[cos_at + k * USED : cos_at + (k + 1) * USED, :]

    coefs = [e] + [e * u for u in unit]
    mask_at = rows.at["mask"][0]

    def put_mask(i, value):
        save[mask_at + 8 * i : mask_at + 8 * i + 8, :] = value

    type_masks(kinds, types, put_mask)

    def read_mask(i):
        return save[mask_at + 8 * i : mask_at + 8 * i + 8, :]

    slot_sums(read_sin, read_cos, coefs, None, read_mask, slots, types, lambda q, v: rows.put(save, "A%d" % q, v))

    def nw(name):
        return narrow.get(nh, name), narrow.get(nl, name)

    def wd(name, first=None, last=None, rsl=slice(None)):
        return tuple(wide.get(r, name)[rsl, first:last] for r in (wh, wl))

    a0 = split(rows.get(save, "A0"))
    av = split(cat([rows.get(save, "A%d" % q) for q in (1, 2, 3)], 1))
    s_one = features[...] + dot3(wd("BT", rsl=slice(0, feat)), a0)
    v = dot3(wd("BT", rsl=slice(feat, 2 * feat)), av)
    uw = dot3(nw("RQT"), split(v))
    turned, mirrored = thirds(uw[0:feat]), thirds(uw[feat : 2 * feat])
    q = turned[0] * mirrored[0] + turned[1] * mirrored[1] + turned[2] * mirrored[2]
    n = jnp.sqrt(mirrored[0] * mirrored[0] + mirrored[1] * mirrored[1] + mirrored[2] * mirrored[2] + 1.0)
    joined = cat([s_one, n], 0)
    h = dot3(wd("CT"), split(joined))
    gate = lax.logistic(h)
    z = h * gate
    dz = gate * (1.0 + h * (1.0 - gate))
    d2z = gate * (1.0 - gate) * (2.0 + h * (1.0 - 2.0 * gate))
    a = dot3(nw("ST"), split(z))
    a2 = a[feat : 2 * feat]
    s_two = s_one + a[0:feat] + a2 * q
    y = dot3(nw("RT"), split(s_two))
    gate = lax.logistic(y)
    dy = gate * (1.0 + y * (1.0 - gate))
    d2y = gate * (1.0 - gate) * (2.0 + y * (1.0 - 2.0 * gate))
    ldy = dy * live
    yb = colmat[...] * ldy
    s2b = dot3(nw("R"), split(yb))
    ab = cat([s2b, s2b * q], 0)
    qb = s2b * a2
    zb = dot3(wd("S"), split(ab))
    hb = zb * dz
    jb = dot3(nw("C"), split(hb))
    s1b = s2b + jb[0:feat]
    nbn = jb[feat : 2 * feat] / n
    uwb = cat(
        [
            cat([qb * mirrored[c] for c in range(3)], 1),
            cat([nbn * mirrored[c] + qb * turned[c] for c in range(3)], 1),
        ],
        0,
    )
    vb = dot3(wd("RQ"), split(uwb))
    for name, value in (
        ("joined", joined), ("ab", ab), ("z", z), ("dz", dz), ("d2z", d2z), ("a2", a2), ("q", q), ("n", n),
        ("s2", s_two), ("yb", yb), ("yc", colmat[...] * live * d2y), ("ldy", ldy), ("s2b", s2b), ("zb", zb),
        ("hb", hb), ("qb", qb), ("nbn", nbn), ("s1b", s1b),
    ):
        rows.put(save, name, value)
    for name, value in (("v", v), ("uw", uw), ("uwb", uwb), ("vb", vb)):
        for c, part in enumerate(thirds(value)):
            rows.put(save, "%s%d" % (name, c), part)
    ab0 = dot3(wd("B", 0, feat), split(s1b))
    abv = thirds(dot3(wd("B", feat, 2 * feat), split(vb)))

    def put(name, q, k, row):
        start = rows.at["%s%d" % (name, q)][0] + k
        save[start : start + 1, :] = row

    tables = [ab0] + abv
    slot_reads(lambda q: tables[q], kinds, read_sin, read_cos, slots, types, put, True)
    sa = [rows.get(save, "sa%d" % q) for q in range(4)]
    sb = [rows.get(save, "sb%d" % q) for q in range(4)]
    z_sum = unit[0] * sa[1] + unit[1] * sa[2] + unit[2] * sa[3]
    x_sum = sb[0] + unit[0] * sb[1] + unit[1] * sb[2] + unit[2] * sb[3]
    rb = e * x_sum + e1 * (sa[0] + z_sum) - ir * e * z_sum
    deltas_bar = [rb * unit[c] + e * ir * sa[c + 1] for c in range(3)]
    pool_partials(deltas_bar, code, lambda j: index[slots + j : slots + j + 1, :], (low, high), scratch, lanes)


def centres_of(bins, bin_total):
    return 0.1 * jnp.sqrt(3600.0 * (bins.astype(f32) + 0.5) / bin_total)


def hist_body(
    depth, bin_total, pool, left, right, from_left, from_right, index, masks, bins,
    next_own, slopes, hist, moved, scratch,
):
    lanes = pool.shape[2]
    slots = index.shape[0] - 8
    code = index[0:slots, :]
    inverse = index[slots + 4 : slots + 5, :]
    mask = masks[0:slots, :]
    for j in range(4):
        kick = (0.5 * time_step * time_step) * pool[j, 6:7, :]
        force = whole((left, right, from_left, from_right), j)
        moved[j, 0:3, :] = pool[j, 0:3, :] + time_step * pool[j, 3:6, :] - kick * force[0:3, :]
    inverse8 = jnp.broadcast_to(inverse, (8, lanes))
    own = []
    for c in range(3):
        row = from_pool([moved[j, c : c + 1, :] for j in range(4)], inverse8, lanes)[0:1, :]
        next_own[c : c + 1, :] = row
        own.append(row)

    def coords(j, c):
        shift = pool_offsets(j, lanes)[c]
        row = moved[j, c : c + 1, :]
        return row if shift is None else row + shift

    deltas, radius = pool_deltas(coords, lambda c: own[c], code, lanes, depth)
    gap = radius - centres_of(bins[...], bin_total)
    kernel = jnp.exp(-gap * gap / sigma_two) * mask
    scale = kernel * gap * (-2.0 / sigma_two) / radius
    for c in range(3):
        slopes[c * slots : (c + 1) * slots, :] = scale * deltas[c]
    sums = scatter_lanes([kernel], bins[...], scratch, bin_total)
    hist[...] = jnp.broadcast_to(sums[0:1, :], hist.shape)


def adjoint_body(atoms_total, hists, target, slopes, index, bins, low, high, scratch):
    lanes = bins.shape[1]
    slots = bins.shape[0]
    code = index[0:slots, :]
    total = jnp.sum(hists[...], axis=0, keepdims=True)
    weights = 2.0 * (total / atoms_total - target[...]) / atoms_total
    picked = lane_take(weights, bins[...])
    deltas_bar = [picked * slopes[c * slots : (c + 1) * slots, :] for c in range(3)]
    pool_partials(deltas_bar, code, lambda j: index[slots + j : slots + j + 1, :], (low, high), scratch, lanes)


def grads_body(
    types, pool, left, right, from_left, from_right, index, save, colmat, phi, filt, nh, nl, wh, wl,
    keep, send, adjoint, after, tangents, grads,
):
    lanes = pool.shape[2]
    slots = index.shape[0] - 8
    feat = colmat.shape[0]
    rows = saved_rows(feat, types, slots)
    narrow = narrow_rows(feat)
    wide = wide_rows(feat, types)
    code = index[0:slots, :]
    inverse8 = jnp.broadcast_to(index[slots + 4 : slots + 5, :], (8, lanes))

    def get(name):
        return rows.get(save, name)

    for j in range(4):
        adjoint[j, :, :] = whole((left, right, from_left, from_right), j)
    probe = [
        [(0.5 * time_step * time_step) * pool[j, 6:7, :] * adjoint[j, c : c + 1, :] for j in range(4)]
        for c in range(3)
    ]
    moves = [
        from_pool(probe[c], code, lanes) - from_pool(probe[c], inverse8, lanes)[0:1, :] for c in range(3)
    ]
    e, e1, e2, ir, kinds = get("e"), get("e1"), get("e2"), get("ir"), get("t")
    unit = [get("u%d" % c) for c in range(3)]
    dr = unit[0] * moves[0] + unit[1] * moves[1] + unit[2] * moves[2]
    du = [(moves[c] - unit[c] * dr) * ir for c in range(3)]
    de = e1 * dr
    sin_at, cos_at = rows.at["sin"][0], rows.at["cos"][0]

    def read_sin(k):
        return save[sin_at + k * USED : sin_at + (k + 1) * USED, :]

    def read_cos(k):
        return save[cos_at + k * USED : cos_at + (k + 1) * USED, :]

    k_rows = STRIDE * types

    def put_sum(q, value):
        tangents[q * k_rows : (q + 1) * k_rows, :] = value

    sin_coef = [de] + [de * unit[c] + e * du[c] for c in range(3)]
    cos_coef = [e * dr] + [e * dr * unit[c] for c in range(3)]
    mask_at = rows.at["mask"][0]

    def read_mask(i):
        return save[mask_at + 8 * i : mask_at + 8 * i + 8, :]

    slot_sums(read_sin, read_cos, sin_coef, cos_coef, read_mask, slots, types, put_sum)

    def nw(name):
        return narrow.get(nh, name), narrow.get(nl, name)

    def wd(name, first=None, last=None, rsl=slice(None)):
        return tuple(wide.get(r, name)[rsl, first:last] for r in (wh, wl))

    da_zero = tangents[0:k_rows, :]
    da_vec = cat([tangents[q * k_rows : (q + 1) * k_rows, :] for q in (1, 2, 3)], 1)
    ds1 = dot3(wd("BT", rsl=slice(0, feat)), split(da_zero))
    dv = dot3(wd("BT", rsl=slice(feat, 2 * feat)), split(da_vec))
    duw = dot3(nw("RQT"), split(dv))
    d_turn, d_mirr = thirds(duw[0:feat]), thirds(duw[feat : 2 * feat])
    turned = [get("uw%d" % c)[0:feat] for c in range(3)]
    mirrored = [get("uw%d" % c)[feat : 2 * feat] for c in range(3)]
    q, n, a2, dz, d2z = get("q"), get("n"), get("a2"), get("dz"), get("d2z")
    s2b, zb, qb, nbn = get("s2b"), get("zb"), get("qb"), get("nbn")
    dq = sum(d_turn[c] * mirrored[c] + turned[c] * d_mirr[c] for c in range(3))
    dn = sum(mirrored[c] * d_mirr[c] for c in range(3)) / n
    dj = cat([ds1, dn], 0)
    dh = dot3(wd("CT"), split(dj))
    dzt = dz * dh
    da = dot3(nw("ST"), split(dzt))
    da2 = da[feat : 2 * feat]
    ds2 = ds1 + da[0:feat] + da2 * q + a2 * dq
    dyt = dot3(nw("RT"), split(ds2))
    dyb = get("yc") * dyt
    ds2b = dot3(nw("R"), split(dyb))
    dab = cat([ds2b, ds2b * q + s2b * dq], 0)
    dqb = ds2b * a2 + s2b * da2
    dzb = dot3(wd("S"), split(dab))
    dhb = dzb * dz + zb * (d2z * dh)
    djb = dot3(nw("C"), split(dhb))
    ds1b = ds2b + djb[0:feat]
    dnbn = (djb[feat : 2 * feat] - nbn * dn) / n
    duwb = cat(
        [
            cat([dqb * mirrored[c] + qb * d_mirr[c] for c in range(3)], 1),
            cat(
                [
                    dnbn * mirrored[c] + nbn * d_mirr[c] + dqb * turned[c] + qb * d_turn[c]
                    for c in range(3)
                ],
                1,
            ),
        ],
        0,
    )
    dvb = dot3(wd("RQ"), split(duwb))

    def both(first, second, third, fourth):
        return -dot3(split(cat([first, second], 1)), split(cat([third, fourth], 1)), NT)

    parts = grads.shape[0]
    share = feat // parts
    rq = both(dv, triple(rows, save, "v"), triple(rows, save, "uwb"), duwb)
    cg = both(dj, get("joined"), get("hb"), dhb)
    sg = both(dzt, get("z"), get("ab"), dab)
    rg = both(ds2, get("s2"), get("yb"), dyb)
    bs = both(da_zero, get("A0"), get("s1b"), ds1b)
    bv = both(da_vec, cat([get("A%d" % i) for i in (1, 2, 3)], 1), triple(rows, save, "vb"), dvb)
    low, high = split(get("ldy") * dyt)
    ones = jnp.ones((16, lanes), bf16)
    col = -(dot1(ones, low, NT) + dot1(ones, high, NT))
    fg, pg = [], []
    for half, value in enumerate((bs, bv)):
        cols = slice(half * feat, (half + 1) * feat)
        total = None
        for t in range(types):
            block = value[STRIDE * t : STRIDE * t + USED, :]
            term = block * phi[t : t + 1, cols]
            total = term if total is None else total + term
            pg.append((half, t, jnp.sum(block * filt[0:USED, cols], axis=0, keepdims=True)))
        fg.append(total)
    base = 7 * share
    place = iota((10, lanes), 1)
    for part in range(parts):
        mine = slice(part * share, (part + 1) * share)
        grads[part, 0:share, :] = rq[mine, 0:feat]
        grads[part, share : 2 * share, :] = rq[mine, feat : 2 * feat]
        grads[part, 2 * share : 4 * share, :] = cg[2 * part * share : 2 * (part + 1) * share, :]
        grads[part, 4 * share : 5 * share, :] = sg[mine, 0:feat]
        grads[part, 5 * share : 6 * share, :] = sg[mine, feat : 2 * feat]
        grads[part, 6 * share : 7 * share, :] = rg[mine, :]
        for half, t, row in pg:
            at = base + half * types + t
            grads[part, at : at + 1, :] = row
        chosen = fg[part // 2]
        rolled = pltpu.roll(chosen, feat // 2, 1)
        here, there = (chosen, rolled) if part % 2 == 0 else (rolled, chosen)
        at = base + 2 * types
        grads[part, at : at + 10, :] = jnp.where(place < feat // 2, here[0:10, :], there[10:20, :])
        grads[part, at + 10 : at + 11, :] = col[0:1, :]
        grads[part, at + 11 :, :] = jnp.zeros((grads.shape[1] - at - 11, lanes), f32)

    odd = lax.axis_index("slab") % 2
    half = grads.shape[1] // 2
    keep[...] = grads[:, pl.ds(pl.multiple_of(odd * half, half), half), :]
    send[...] = grads[:, pl.ds(pl.multiple_of((1 - odd) * half, half), half), :]
    for c in range(3):
        after[c * slots : (c + 1) * slots, :] = du[c]
        after[4 * slots + (c + 1) * feat : 4 * slots + (c + 2) * feat, :] = dvb[:, c * lanes : (c + 1) * lanes]
    after[3 * slots : 4 * slots, :] = dr
    after[4 * slots : 4 * slots + feat, :] = ds1b


def moves_body(types, index, save, after, wh, wl, low, high, sums, scratch):
    lanes = index.shape[1]
    slots = index.shape[0] - 8
    feat = lanes
    rows = saved_rows(feat, types, slots)
    wide = wide_rows(feat, types)
    code = index[0:slots, :]

    def get(name):
        return rows.get(save, name)

    def wd(name, first, last):
        return tuple(wide.get(r, name)[:, first:last] for r in (wh, wl))

    e, e1, e2, ir, kinds = get("e"), get("e1"), get("e2"), get("ir"), get("t")
    unit = [get("u%d" % c) for c in range(3)]
    du = [after[c * slots : (c + 1) * slots, :] for c in range(3)]
    dr = after[3 * slots : 4 * slots, :]
    de, de1, dir_ = e1 * dr, e2 * dr, -ir * ir * dr
    sin_at, cos_at = rows.at["sin"][0], rows.at["cos"][0]

    def read_sin(k):
        return save[sin_at + k * USED : sin_at + (k + 1) * USED, :]

    def read_cos(k):
        return save[cos_at + k * USED : cos_at + (k + 1) * USED, :]

    ds1b = after[4 * slots : 4 * slots + feat, :]
    dvb = cat([after[4 * slots + (c + 1) * feat : 4 * slots + (c + 2) * feat, :] for c in range(3)], 1)
    dab0 = dot3(wd("B", 0, feat), split(ds1b))
    dabv = thirds(dot3(wd("B", feat, 2 * feat), split(dvb)))
    tables = [dab0] + dabv

    def put(name, q, k, row):
        start = (0 if name == "sa" else 4 * slots) + q * slots + k
        sums[start : start + 1, :] = row

    slot_reads(lambda q: tables[q], kinds, read_sin, read_cos, slots, types, put, False)
    sa = [get("sa%d" % q) for q in range(4)]
    sb = [get("sb%d" % q) for q in range(4)]
    sd = [get("sd%d" % q) for q in range(4)]
    dsa = [sb[q] * dr + sums[q * slots : (q + 1) * slots, :] for q in range(4)]
    dsb = [
        sums[(4 + q) * slots : (5 + q) * slots, :] - sd[q] * dr for q in range(4)
    ]
    z_sum = sum(unit[c] * sa[c + 1] for c in range(3))
    x_sum = sb[0] + sum(unit[c] * sb[c + 1] for c in range(3))
    dz_sum = sum(du[c] * sa[c + 1] + unit[c] * dsa[c + 1] for c in range(3))
    dx_sum = dsb[0] + sum(du[c] * sb[c + 1] + unit[c] * dsb[c + 1] for c in range(3))
    rb = e * x_sum + e1 * (sa[0] + z_sum) - ir * e * z_sum
    drb = (
        de * x_sum + e * dx_sum + de1 * (sa[0] + z_sum) + e1 * (dsa[0] + dz_sum)
        - (dir_ * e + ir * de) * z_sum - ir * e * dz_sum
    )
    deltas_bar = [
        drb * unit[c] + rb * du[c] + (de * ir + e * dir_) * sa[c + 1] + e * ir * dsa[c + 1]
        for c in range(3)
    ]
    pool_partials(deltas_bar, code, lambda j: index[slots + j : slots + j + 1, :], (low, high), scratch, lanes)


def last_body(
    types, parts, atoms_total, mine, other, adjoint, left, right, index, slope, hidden_t, table_t, spreader, next_own,
    next_out, adj, enc, spr, fil, rot, ref, com, spl, rea, col, total,
):
    next_out[...] = next_own[...]
    odd = lax.axis_index("slab") % 2
    half = mine.shape[0]
    total[pl.ds(pl.multiple_of(odd * half, half), half), :] = mine[...]
    total[pl.ds(pl.multiple_of((1 - odd) * half, half), half), :] = other[...]
    lanes = adjoint.shape[2]
    slots = index.shape[0] - 8
    feat = lanes
    share = feat // parts
    inverse8 = jnp.broadcast_to(index[slots + 4 : slots + 5, :], (8, lanes))
    for c in range(3):
        rows = [
            atoms_total * (adjoint[j, c : c + 1, :] - (left, right)[j % 2][j // 2, c : c + 1, :]) for j in range(4)
        ]
        adj[c : c + 1, :] = from_pool(rows, inverse8, lanes)[0:1, :]
    rot[...] = total[0:share, :]
    ref[...] = total[share : 2 * share, :]
    com[...] = total[2 * share : 4 * share, :]
    spl[:, 0:feat] = total[4 * share : 5 * share, :]
    spl[:, feat : 2 * feat] = total[5 * share : 6 * share, :]
    rea[...] = total[6 * share : 7 * share, :]
    base = 7 * share
    phib = cat([total[base : base + types, :], total[base + types : base + 2 * types, :]], 1)
    at = base + 2 * types
    block = total[at : at + 10, :]
    fil[0:10, :] = block[:, 0 : feat // 2]
    fil[10:20, :] = pltpu.roll(block, feat // 2, 1)[:, 0 : feat // 2]
    col_row = total[at + 10 : at + 11, :]
    spare = jnp.zeros((types, 2 * feat), f32)
    pre_bar = dot3(split(cat([phib, spare], 0)), split(spreader[...]), NT)[0:types] * slope[...]
    here = pl.ds(pl.multiple_of(lax.axis_index("cross") * share, share), share)
    rest = jnp.zeros((lanes - types, feat), f32)
    spr[...] = dot3(split(hidden_t[here, :]), split(cat([phib, cat([rest, rest], 1)], 0)))
    enc[...] = dot3(split(table_t[here, :]), split(cat([pre_bar, rest], 0)))
    for part in range(parts):
        @pl.when(lax.axis_index("cross") == part)
        def _():
            col[...] = col_row[:, part * share : (part + 1) * share]


def shift(x, axis, step):
    count = lax.axis_size(axis)
    return lax.ppermute(x, axis, [(i, (i + step) % count) for i in range(count)])


def both_ways(first, second, axis):
    return shift(first, axis, 1), shift(second, axis, -1)


def corner_sum(low, high):
    left, right = call(turn_body, [(low.shape, f32)] * 2, low, high, *both_ways(high, low, "slab"))
    return (left, right) + both_ways(right, left, "cross")


def swap(x, axis, bit):
    return lax.ppermute(x, axis, [(i, i ^ bit) for i in range(lax.axis_size(axis))])


def halve(bit, x, other, keep, send):
    mine = (lax.axis_index("cross") // bit) % 2
    shape = (x.shape[0] // 2, 2) + x.shape[1:]
    x, other = x.reshape(shape), other.reshape(shape)
    for ref, side in ((keep, mine), (send, 1 - mine)):
        value = x[:, pl.ds(side, 1)] + other[:, pl.ds(side, 1)]
        ref[...] = value.reshape(ref.shape)


def halve_hold_body(bit, x, other, low, high, keep, send, low_out, high_out):
    halve(bit, x, other, keep, send)
    low_out[...] = low[...]
    high_out[...] = high[...]


def halve_turn_body(bit, x, other, low, high, from_down, from_up, keep, send, left, right):
    halve(bit, x, other, keep, send)
    turn_body(low, high, from_down, from_up, left, right)


def add_body(x, other, out):
    out[...] = x[...] + other[...]


def add_two_body(x, other, side, from_side, out, total):
    add_body(x, other, out)
    add_body(side, from_side, total)


def reduce_all(keep, send, low, high):
    slab_count, cross_count = lax.axis_size("slab"), lax.axis_size("cross")
    group = (low.shape, f32)
    other = swap(send, "slab", 1)
    bit, step, pieces = 1, 0, None
    while bit < cross_count:
        half = ((keep.shape[0] // 2,) + keep.shape[1:], f32)
        if step == 0:
            keep, send, low, high = call(
                functools.partial(halve_hold_body, bit), [half, half, group, group], keep, other, low, high
            )
            from_down, from_up = both_ways(high, low, "slab")
        elif step == 1:
            keep, send, left, right = call(
                functools.partial(halve_turn_body, bit), [half, half, group, group],
                keep, other, low, high, from_down, from_up,
            )
            pieces = (left, right) + both_ways(right, left, "cross")
        else:
            raise NotImplementedError
        other = swap(send, "cross", bit)
        bit, step = 2 * bit, step + 1
    x, other = keep[0], other[0]
    left, right, from_left, from_right = pieces
    waiting, sides = [(left, from_left), (right, from_right)], []

    def add(x, other):
        shapes = [(x.shape, f32)]
        if waiting:
            x, side = call(add_two_body, shapes + [group], x, other, *waiting.pop(0))
            sides.append(side)
            return x
        return call(add_body, shapes, x, other)[0]

    bit = 2
    while bit < slab_count:
        x = add(x, other)
        other = swap(x, "slab", bit)
        bit *= 2
    x = add(x, other)
    while waiting:
        sides += call(add_body, [group], *waiting.pop(0))
    return x, swap(x, "slab", 1), sides


def device_step(
    positions, velocities, inverse_mass, species, type_table, neighbours, slot_count, atom_count,
    pair_bins, send_list, target, encoder, spreader, filters, rotator, reflector, combiner, splitter,
    readout, collector,
):
    lanes = positions.shape[1]
    slots = neighbours.shape[1]
    types, feat = type_table.shape
    bin_total = target.shape[0]
    slab_count, cross_count = lax.axis_size("slab"), lax.axis_size("cross")
    devices = slab_count * cross_count
    atoms_total = float(lanes * devices)
    depth = 1.6 * (lanes // 16)
    parts = cross_count
    row = lambda x: x.reshape(1, x.shape[0])
    i32 = jnp.int32
    vm, dma = pltpu.VMEM, pltpu.SemaphoreType.DMA
    narrow, wide = narrow_rows(feat).total, wide_rows(feat, types).total
    group = ((2, 8, lanes), f32)
    pool_shape = ((4, 8, lanes), f32)
    pair_scratch = vm((16 * slots, lanes), f32)
    low, high, own_rows, send = call(
        offer_body, [group, group, ((8, lanes), f32), ((8, lanes), i32)],
        *in_hbm(positions, velocities, row(inverse_mass), row(species), send_list),
        specs=[HB] * 5,
        scratch=[
            vm((3, lanes), f32), vm((3, lanes), f32), vm((1, lanes), f32), vm((1, lanes), i32),
            vm(send_list.shape, i32), dma((5,)),
        ],
    )
    colmat, nh, nl, wh, wl, phi, slope, hidden_t, table_t, filt, spreader_in = call(
        weights_body,
        [
            ((feat, lanes), f32), ((narrow, feat), bf16), ((narrow, feat), bf16), ((wide, 2 * feat), bf16),
            ((wide, 2 * feat), bf16), ((types, 2 * feat), f32), ((types, feat), f32), ((feat, lanes), f32),
            ((feat, lanes), f32), ((STRIDE, 2 * feat), f32), (spreader.shape, f32),
        ],
        *in_hbm(
            type_table, encoder, spreader, filters, rotator, reflector, combiner, splitter, readout,
            row(collector),
        ),
        specs=[HB] * 10,
        scratch=[
            vm(type_table.shape, f32), vm(encoder.shape, f32), vm(filters.shape, f32), vm(rotator.shape, f32),
            vm(reflector.shape, f32), vm(combiner.shape, f32), vm(splitter.shape, f32), vm(readout.shape, f32),
            vm((1, feat), f32), dma((10,)),
        ],
    )
    index, masks, features, bins, goal = call(
        index_body,
        [
            ((slots + 8, lanes), i32), ((slots + 8, lanes), f32), ((feat, lanes), f32), ((slots, lanes), i32),
            ((1, bin_total), f32),
        ],
        *in_hbm(neighbours.T, row(slot_count), pair_bins.T, row(target)),
        atom_count, send, own_rows, table_t,
        specs=[HB] * 4 + [SM] + [VM] * 3,
        scratch=[vm((slots, lanes), i32), vm((1, lanes), i32), dma((4,))],
    )
    pieces = corner_sum(low, high)
    save_rows = saved_rows(feat, types, slots).total
    low, high, pool, save = call(
        functools.partial(force_body, types, depth),
        [group, group, pool_shape, ((save_rows, lanes), f32)],
        *pieces, own_rows, index, masks, features, colmat, nh, nl, wh, wl,
        scratch=[pair_scratch],
    )
    pieces = corner_sum(low, high)
    next_positions, slopes, hist = call(
        functools.partial(hist_body, depth, bin_total),
        [((3, lanes), f32), ((3 * slots, lanes), f32), ((devices, bin_total), f32)],
        pool, *pieces, index, masks, bins,
        scratch=[vm((4, 8, lanes), f32), pair_scratch],
    )
    hists = lax.all_to_all(hist.reshape(devices, 1, bin_total), ("slab", "cross"), 0, 0)
    low, high = call(
        functools.partial(adjoint_body, atoms_total), [group, group],
        hists.reshape(devices, bin_total), goal, slopes, index, bins,
        scratch=[pair_scratch],
    )
    pieces = corner_sum(low, high)
    half_grads = ((parts, feat, lanes), f32)
    keep, send, adjoint, after = call(
        functools.partial(grads_body, types),
        [half_grads, half_grads, pool_shape, ((4 * slots + 4 * feat, lanes), f32)],
        pool, *pieces, index, save, colmat, phi, filt, nh, nl, wh, wl,
        scratch=[vm((4 * STRIDE * types, lanes), f32), vm((parts, 2 * feat, lanes), f32)],
    )
    low, high = call(
        functools.partial(moves_body, types), [group, group], index, save, after, wh, wl,
        scratch=[vm((8 * slots, lanes), f32), pair_scratch],
    )
    mine, other, sides = reduce_all(keep, send, low, high)
    share = feat // parts
    results = call(
        functools.partial(last_body, types, parts, atoms_total),
        [
            ((3, lanes), f32), ((3, lanes), f32), ((share, feat), f32), ((share, 2 * feat), f32),
            ((filters.shape[0], 2 * feat // parts), f32), ((share, feat), f32), ((share, feat), f32),
            ((2 * share, feat), f32), ((share, 2 * feat), f32), ((share, feat), f32), ((1, share), f32),
        ],
        mine, other, adjoint, *sides, index, slope, hidden_t, table_t, spreader_in, next_positions,
        scratch=[vm((2 * feat, lanes), f32)],
        keep=False,
    )
    return tuple(results[:10]) + (results[10].reshape(share),)


def solution(mesh):
    both = ("slab", "cross")
    in_specs = (
        P(None, both), P(None, both), P(both), P(both), P(), P(both, None), P(both), P(both), P(both, None),
        P("slab", "cross", None),
    ) + (P(),) * 10
    out_specs = (
        P(None, both), P(None, both), P("cross", None), P("cross", None), P(None, "cross"), P("cross", None),
        P("cross", None), P("cross", None), P("cross", None), P("cross", None), P("cross"),
    )
    return jax.shard_map(device_step, mesh=mesh, in_specs=in_specs, out_specs=out_specs, check_vma=False)
```

profile of v0, /device:TPU:0, one launch (start us, length us, event | category | flops | bytes accessed | tf_op | source)
XLA Modules:
  0.0 81.7 jit_solution(15414630319830680519)
XLA Ops:
  1.6 3.4 %collective-permute-start.1 = (f32[2,8,128]{2,1,0:T(8,128)S(1)}, f32[2,8,128]{2,1,0:T(8,128)S(1)}, u32[]{:S(2)}, u32[]{:S(2)}) collective-permute-start(f32[2,8,128]{2,1,0:T(8,128)S(1)} %get-tuple-element.75.low), channel_id=1, source_target_pairs={{0,28},{4,0},{8,4},{12,8},{16,12},{20,16},{24,20},{28,24},{1,29},{... | collective-permute-start | bytes 24584 | tf_op jit(solution)/shard_map/ppermute | solution.py:908
  5.0 1.4 %collective-permute-done.1.from_up = f32[2,8,128]{2,1,0:T(8,128)S(1)} collective-permute-done((f32[2,8,128]{2,1,0:T(8,128)S(1)}, f32[2,8,128]{2,1,0:T(8,128)S(1)}, u32[]{:S(2)}, u32[]{:S(2)}) %collective-permute-start.1) | collective-permute-done | bytes 8224 | tf_op jit(solution)/shard_map/ppermute | solution.py:908
  6.4 2.6 %collective-permute-done.from_down = f32[2,8,128]{2,1,0:T(8,128)S(1)} collective-permute-done((f32[2,8,128]{2,1,0:T(8,128)S(1)}, f32[2,8,128]{2,1,0:T(8,128)S(1)}, u32[]{:S(2)}, u32[]{:S(2)}) %collective-permute-start) | collective-permute-done | bytes 8224 | tf_op jit(solution)/shard_map/ppermute | solution.py:908
  9.0 3.6 %collective-permute-start.3 = (f32[2,8,128]{2,1,0:T(8,128)S(1)}, f32[2,8,128]{2,1,0:T(8,128)S(1)}, u32[]{:S(2)}, u32[]{:S(2)}) collective-permute-start(f32[2,8,128]{2,1,0:T(8,128)S(1)} %get-tuple-element.77.left), channel_id=1, source_target_pairs={{0,3},{1,0},{2,1},{3,2},{4,7},{5,4},{6,5},{7,6},{8,11},{9,8},{10,9... | collective-permute-start | bytes 24584 | tf_op jit(solution)/shard_map/ppermute | solution.py:908
  13.2 1.9 %shard_map.277 = (f32[128,128]{1,0:T(8,128)S(1)}, bf16[1024,128]{1,0:T(8,128)(2,1)S(1)}, bf16[1024,128]{1,0:T(8,128)(2,1)S(1)}, bf16[896,256]{1,0:T(8,128)(2,1)S...) custom-call(f32[8,128]{1,0:T(8,128)} %table_h.1, ...), custom_call_target="tpu_custom_call" | custom-call | tf_op jit(solution)/shard_map/pallas_call | solution.py:31
  16.2 1.8 %collective-permute-done.2.from_left = f32[2,8,128]{2,1,0:T(8,128)S(1)} collective-permute-done((f32[2,8,128]{2,1,0:T(8,128)S(1)}, f32[2,8,128]{2,1,0:T(8,128)S(1)}, u32[]{:S(2)}, u32[]{:S(2)}) %collective-permute-start.2) | collective-permute-done | bytes 8224 | tf_op jit(solution)/shard_map/ppermute | solution.py:908
  18.0 4.1 %shard_map.279 = (f32[2,8,128]{2,1,0:T(8,128)S(1)}, f32[2,8,128]{2,1,0:T(8,128)S(1)}, f32[4,8,128]{2,1,0:T(8,128)S(1)}, f32[8000,128]{1,0:T(8,128)S(1)}) custom-call(f32[2,8,128]{2,1,0:T(8,128)S(1)} %get-tuple-element.77.left, f32[2,8,128]{2,1,0:T(8,128)S(1)} %get-tuple-element.78.right, f32[2,8,128]{2,1,0:T(8,128)S(1)} %collective-permute-done.2.from_left, ...), custom_call_target="tpu_custom_call" | custom-call | tf_op jit(solution)/shard_map/pallas_call | solution.py:31
  23.5 2.6 %collective-permute-done.4.from_down = f32[2,8,128]{2,1,0:T(8,128)S(1)} collective-permute-done((f32[2,8,128]{2,1,0:T(8,128)S(1)}, f32[2,8,128]{2,1,0:T(8,128)S(1)}, u32[]{:S(2)}, u32[]{:S(2)}) %collective-permute-start.4) | collective-permute-done | bytes 8224 | tf_op jit(solution)/shard_map/ppermute | solution.py:908
  26.1 2.0 %collective-permute-start.7 = (f32[2,8,128]{2,1,0:T(8,128)S(1)}, f32[2,8,128]{2,1,0:T(8,128)S(1)}, u32[]{:S(2)}, u32[]{:S(2)}) collective-permute-start(f32[2,8,128]{2,1,0:T(8,128)S(1)} %get-tuple-element.93.left), channel_id=1, source_target_pairs={{0,3},{1,0},{2,1},{3,2},{4,7},{5,4},{6,5},{7,6},{8,11},{9,8},{10,9... | collective-permute-start | bytes 24584 | tf_op jit(solution)/shard_map/ppermute | solution.py:908
  28.1 1.6 %collective-permute-done.7.from_right = f32[2,8,128]{2,1,0:T(8,128)S(1)} collective-permute-done((f32[2,8,128]{2,1,0:T(8,128)S(1)}, f32[2,8,128]{2,1,0:T(8,128)S(1)}, u32[]{:S(2)}, u32[]{:S(2)}) %collective-permute-start.7) | collective-permute-done | bytes 8224 | tf_op jit(solution)/shard_map/ppermute | solution.py:908
  29.8 3.8 %collective-permute-done.6.from_left = f32[2,8,128]{2,1,0:T(8,128)S(1)} collective-permute-done((f32[2,8,128]{2,1,0:T(8,128)S(1)}, f32[2,8,128]{2,1,0:T(8,128)S(1)}, u32[]{:S(2)}, u32[]{:S(2)}) %collective-permute-start.6) | collective-permute-done | bytes 8224 | tf_op jit(solution)/shard_map/ppermute | solution.py:908
  34.0 8.9 %all_to_all.5 = f32[32,1,128]{2,1,0:T(1,128)S(1)} all-to-all(f32[32,1,128]{2,1,0:T(1,128)S(1)} %bitcast.17), channel_id=1, replica_groups=mesh['slab'=8,'cross'=4] {'slab','cross'}, dimensions={0} | all-to-all | bytes 32768 | tf_op jit(solution)/shard_map/all_to_all | solution.py:1072
  44.6 2.7 %collective-permute-done.8.from_down = f32[2,8,128]{2,1,0:T(8,128)S(1)} collective-permute-done((f32[2,8,128]{2,1,0:T(8,128)S(1)}, f32[2,8,128]{2,1,0:T(8,128)S(1)}, u32[]{:S(2)}, u32[]{:S(2)}) %collective-permute-start.8) | collective-permute-done | bytes 8224 | tf_op jit(solution)/shard_map/ppermute | solution.py:908
  47.9 1.5 %collective-permute-start.10 = (f32[2,8,128]{2,1,0:T(8,128)S(1)}, f32[2,8,128]{2,1,0:T(8,128)S(1)}, u32[]{:S(2)}, u32[]{:S(2)}) collective-permute-start(f32[2,8,128]{2,1,0:T(8,128)S(1)} %get-tuple-element.102.right), channel_id=1, source_target_pairs={{0,1},{1,2},{2,3},{3,0},{4,5},{5,6},{6,7},{7,4},{8,9},{9,10},{10,1... | collective-permute-start | bytes 24584 | tf_op jit(solution)/shard_map/ppermute | solution.py:908
  49.3 1.6 %collective-permute-done.11.from_right = f32[2,8,128]{2,1,0:T(8,128)S(1)} collective-permute-done((f32[2,8,128]{2,1,0:T(8,128)S(1)}, f32[2,8,128]{2,1,0:T(8,128)S(1)}, u32[]{:S(2)}, u32[]{:S(2)}) %collective-permute-start.11) | collective-permute-done | bytes 8224 | tf_op jit(solution)/shard_map/ppermute | solution.py:908
  51.0 2.3 %collective-permute-done.10.from_left = f32[2,8,128]{2,1,0:T(8,128)S(1)} collective-permute-done((f32[2,8,128]{2,1,0:T(8,128)S(1)}, f32[2,8,128]{2,1,0:T(8,128)S(1)}, u32[]{:S(2)}, u32[]{:S(2)}) %collective-permute-start.10) | collective-permute-done | bytes 8224 | tf_op jit(solution)/shard_map/ppermute | solution.py:908
  53.3 4.1 %shard_map.284 = (f32[4,128,128]{2,1,0:T(8,128)S(1)}, f32[4,128,128]{2,1,0:T(8,128)S(1)}, f32[4,8,128]{2,1,0:T(8,128)S(1)}, f32[576,128]{1,0:T(8,128)S(1)}) custom-call(f32[4,8,128]{2,1,0:T(8,128)S(1)} %get-tuple-element.90.pool, f32[2,8,128]{2,1,0:T(8,128)S(1)} %get-tuple-element.101.left, f32[2,8,128]{2,1,0:T(8,128)S(1)} %get-tuple-element.102.right, ...), custom_call_target="tpu_custom_call" | custom-call | tf_op jit(solution)/shard_map/pallas_call | solution.py:31
  60.9 2.6 %collective-permute-done.14.from_down = f32[2,8,128]{2,1,0:T(8,128)S(1)} collective-permute-done((f32[2,8,128]{2,1,0:T(8,128)S(1)}, f32[2,8,128]{2,1,0:T(8,128)S(1)}, u32[]{:S(2)}, u32[]{:S(2)}) %collective-permute-start.14) | collective-permute-done | bytes 8224 | tf_op jit(solution)/shard_map/ppermute | solution.py:908
  63.5 1.2 %collective-permute-done.13.other = f32[2,128,128]{2,1,0:T(8,128)S(1)} collective-permute-done((f32[2,128,128]{2,1,0:T(8,128)S(1)}, f32[2,128,128]{2,1,0:T(8,128)S(1)}, u32[]{:S(2)}, u32[]{:S(2)}) %collective-permute-start.13) | collective-permute-done | bytes 131104 | tf_op jit(solution)/shard_map/ppermute | solution.py:921
  65.4 5.0 %collective-permute-done.17.from_side = f32[2,8,128]{2,1,0:T(8,128)S(1)} collective-permute-done((f32[2,8,128]{2,1,0:T(8,128)S(1)}, f32[2,8,128]{2,1,0:T(8,128)S(1)}, u32[]{:S(2)}, u32[]{:S(2)}) %collective-permute-start.17) | collective-permute-done | bytes 8224 | tf_op jit(solution)/shard_map/ppermute | solution.py:908
  72.0 3.0 %collective-permute-done.19.from_side = f32[2,8,128]{2,1,0:T(8,128)S(1)} collective-permute-done((f32[2,8,128]{2,1,0:T(8,128)S(1)}, f32[2,8,128]{2,1,0:T(8,128)S(1)}, u32[]{:S(2)}, u32[]{:S(2)}) %collective-permute-start.19) | collective-permute-done | bytes 8224 | tf_op jit(solution)/shard_map/ppermute | solution.py:908
  75.0 1.4 %collective-permute-start.20 = (f32[128,128]{1,0:T(8,128)S(1)}, f32[128,128]{1,0:T(8,128)S(1)}, u32[]{:S(2)}, u32[]{:S(2)}) collective-permute-start(f32[128,128]{1,0:T(8,128)S(1)} %get-tuple-element.120.x), channel_id=1, source_target_pairs={{0,16},{4,20},{8,24},{12,28},{16,0},{20,4},{24,8},{28,12},{1,17},{... | collective-permute-start | bytes 196616 | tf_op jit(solution)/shard_map/ppermute | solution.py:921
  76.4 2.9 %collective-permute-done.20.other = f32[128,128]{1,0:T(8,128)S(1)} collective-permute-done((f32[128,128]{1,0:T(8,128)S(1)}, f32[128,128]{1,0:T(8,128)S(1)}, u32[]{:S(2)}, u32[]{:S(2)}) %collective-permute-start.20) | collective-permute-done | bytes 65568 | tf_op jit(solution)/shard_map/ppermute | solution.py:921
  79.4 1.2 %collective-permute-done.21.other = f32[128,128]{1,0:T(8,128)S(1)} collective-permute-done((f32[128,128]{1,0:T(8,128)S(1)}, f32[128,128]{1,0:T(8,128)S(1)}, u32[]{:S(2)}, u32[]{:S(2)}) %collective-permute-start.21) | collective-permute-done | bytes 65568 | tf_op jit(solution)/shard_map/ppermute | solution.py:921
  (38 shorter events, 13.0 us)
Async XLA Ops:
  1.6 4.8 %collective-permute-start.1 = (f32[2,8,128]{2,1,0:T(8,128)S(1)}, f32[2,8,128]{2,1,0:T(8,128)S(1)}, u32[]{:S(2)}, u32[]{:S(2)}) collective-permute-start(f32[2,8,128]{2,1,0:T(8,128)S(1)} %get-tuple-element.75.low), channel_id=1, source_target_pairs={{0,28},{4,0},{8,4},{12,8},{16,12},{20,16},{24,20},{28,24},{1,29},{... | collective-permute-start | bytes 24584 | tf_op jit(solution)/shard_map/ppermute | solution.py:908
  5.0 4.0 %collective-permute-start = (f32[2,8,128]{2,1,0:T(8,128)S(1)}, f32[2,8,128]{2,1,0:T(8,128)S(1)}, u32[]{:S(2)}, u32[]{:S(2)}) collective-permute-start(f32[2,8,128]{2,1,0:T(8,128)S(1)} %get-tuple-element.76.high), channel_id=1, source_target_pairs={{0,4},{4,8},{8,12},{12,16},{16,20},{20,24},{24,28},{28,0},{1,5},{5... | collective-permute-start | bytes 24584 | tf_op jit(solution)/shard_map/ppermute | solution.py:908
  9.0 7.2 %collective-permute-start.3 = (f32[2,8,128]{2,1,0:T(8,128)S(1)}, f32[2,8,128]{2,1,0:T(8,128)S(1)}, u32[]{:S(2)}, u32[]{:S(2)}) collective-permute-start(f32[2,8,128]{2,1,0:T(8,128)S(1)} %get-tuple-element.77.left), channel_id=1, source_target_pairs={{0,3},{1,0},{2,1},{3,2},{4,7},{5,4},{6,5},{7,6},{8,11},{9,8},{10,9... | collective-permute-start | bytes 24584 | tf_op jit(solution)/shard_map/ppermute | solution.py:908
  12.6 5.4 %collective-permute-start.2 = (f32[2,8,128]{2,1,0:T(8,128)S(1)}, f32[2,8,128]{2,1,0:T(8,128)S(1)}, u32[]{:S(2)}, u32[]{:S(2)}) collective-permute-start(f32[2,8,128]{2,1,0:T(8,128)S(1)} %get-tuple-element.78.right), channel_id=1, source_target_pairs={{0,1},{1,2},{2,3},{3,0},{4,5},{5,6},{6,7},{7,4},{8,9},{9,10},{10,1... | collective-permute-start | bytes 24584 | tf_op jit(solution)/shard_map/ppermute | solution.py:908
  22.1 1.4 %collective-permute-start.5 = (f32[2,8,128]{2,1,0:T(8,128)S(1)}, f32[2,8,128]{2,1,0:T(8,128)S(1)}, u32[]{:S(2)}, u32[]{:S(2)}) collective-permute-start(f32[2,8,128]{2,1,0:T(8,128)S(1)} %get-tuple-element.91.low), channel_id=1, source_target_pairs={{0,28},{4,0},{8,4},{12,8},{16,12},{20,16},{24,20},{28,24},{1,29},{... | collective-permute-start | bytes 24584 | tf_op jit(solution)/shard_map/ppermute | solution.py:908
  22.1 4.0 %collective-permute-start.4 = (f32[2,8,128]{2,1,0:T(8,128)S(1)}, f32[2,8,128]{2,1,0:T(8,128)S(1)}, u32[]{:S(2)}, u32[]{:S(2)}) collective-permute-start(f32[2,8,128]{2,1,0:T(8,128)S(1)} %get-tuple-element.92.high), channel_id=1, source_target_pairs={{0,4},{4,8},{8,12},{12,16},{16,20},{20,24},{24,28},{28,0},{1,5},{5... | collective-permute-start | bytes 24584 | tf_op jit(solution)/shard_map/ppermute | solution.py:908
  26.1 3.7 %collective-permute-start.7 = (f32[2,8,128]{2,1,0:T(8,128)S(1)}, f32[2,8,128]{2,1,0:T(8,128)S(1)}, u32[]{:S(2)}, u32[]{:S(2)}) collective-permute-start(f32[2,8,128]{2,1,0:T(8,128)S(1)} %get-tuple-element.93.left), channel_id=1, source_target_pairs={{0,3},{1,0},{2,1},{3,2},{4,7},{5,4},{6,5},{7,6},{8,11},{9,8},{10,9... | collective-permute-start | bytes 24584 | tf_op jit(solution)/shard_map/ppermute | solution.py:908
  28.1 5.4 %collective-permute-start.6 = (f32[2,8,128]{2,1,0:T(8,128)S(1)}, f32[2,8,128]{2,1,0:T(8,128)S(1)}, u32[]{:S(2)}, u32[]{:S(2)}) collective-permute-start(f32[2,8,128]{2,1,0:T(8,128)S(1)} %get-tuple-element.94.right), channel_id=1, source_target_pairs={{0,1},{1,2},{2,3},{3,0},{4,5},{5,6},{6,7},{7,4},{8,9},{9,10},{10,1... | collective-permute-start | bytes 24584 | tf_op jit(solution)/shard_map/ppermute | solution.py:908
  43.2 1.4 %collective-permute-start.9 = (f32[2,8,128]{2,1,0:T(8,128)S(1)}, f32[2,8,128]{2,1,0:T(8,128)S(1)}, u32[]{:S(2)}, u32[]{:S(2)}) collective-permute-start(f32[2,8,128]{2,1,0:T(8,128)S(1)} %get-tuple-element.99.low), channel_id=1, source_target_pairs={{0,28},{4,0},{8,4},{12,8},{16,12},{20,16},{24,20},{28,24},{1,29},{... | collective-permute-start | bytes 24584 | tf_op jit(solution)/shard_map/ppermute | solution.py:908
  43.3 4.0 %collective-permute-start.8 = (f32[2,8,128]{2,1,0:T(8,128)S(1)}, f32[2,8,128]{2,1,0:T(8,128)S(1)}, u32[]{:S(2)}, u32[]{:S(2)}) collective-permute-start(f32[2,8,128]{2,1,0:T(8,128)S(1)} %get-tuple-element.100.high), channel_id=1, source_target_pairs={{0,4},{4,8},{8,12},{12,16},{16,20},{20,24},{24,28},{28,0},{1,5},{5... | collective-permute-start | bytes 24584 | tf_op jit(solution)/shard_map/ppermute | solution.py:908
  47.3 3.7 %collective-permute-start.11 = (f32[2,8,128]{2,1,0:T(8,128)S(1)}, f32[2,8,128]{2,1,0:T(8,128)S(1)}, u32[]{:S(2)}, u32[]{:S(2)}) collective-permute-start(f32[2,8,128]{2,1,0:T(8,128)S(1)} %get-tuple-element.101.left), channel_id=1, source_target_pairs={{0,3},{1,0},{2,1},{3,2},{4,7},{5,4},{6,5},{7,6},{8,11},{9,8},{10,9... | collective-permute-start | bytes 24584 | tf_op jit(solution)/shard_map/ppermute | solution.py:908
  47.9 5.4 %collective-permute-start.10 = (f32[2,8,128]{2,1,0:T(8,128)S(1)}, f32[2,8,128]{2,1,0:T(8,128)S(1)}, u32[]{:S(2)}, u32[]{:S(2)}) collective-permute-start(f32[2,8,128]{2,1,0:T(8,128)S(1)} %get-tuple-element.102.right), channel_id=1, source_target_pairs={{0,1},{1,2},{2,3},{3,0},{4,5},{5,6},{6,7},{7,4},{8,9},{9,10},{10,1... | collective-permute-start | bytes 24584 | tf_op jit(solution)/shard_map/ppermute | solution.py:908
  57.4 1.6 %collective-permute-start.12 = (f32[4,128,128]{2,1,0:T(8,128)S(1)}, f32[4,128,128]{2,1,0:T(8,128)S(1)}, u32[]{:S(2)}, u32[]{:S(2)}) collective-permute-start(f32[4,128,128]{2,1,0:T(8,128)S(1)} %get-tuple-element.107), channel_id=1, source_target_pairs={{0,4},{4,0},{8,12},{12,8},{16,20},{20,16},{24,28},{28,24},{1,5},{5... | collective-permute-start | bytes 786440 | tf_op jit(solution)/shard_map/ppermute | solution.py:921
  59.1 5.7 %collective-permute-start.13 = (f32[2,128,128]{2,1,0:T(8,128)S(1)}, f32[2,128,128]{2,1,0:T(8,128)S(1)}, u32[]{:S(2)}, u32[]{:S(2)}) collective-permute-start(f32[2,128,128]{2,1,0:T(8,128)S(1)} %get-tuple-element.112), channel_id=1, source_target_pairs={{0,1},{1,0},{2,3},{3,2},{4,5},{5,4},{6,7},{7,6},{8,9},{9,8},{10,11... | collective-permute-start | bytes 393224 | tf_op jit(solution)/shard_map/ppermute | solution.py:921
  59.1 1.7 %collective-permute-start.15 = (f32[2,8,128]{2,1,0:T(8,128)S(1)}, f32[2,8,128]{2,1,0:T(8,128)S(1)}, u32[]{:S(2)}, u32[]{:S(2)}) collective-permute-start(f32[2,8,128]{2,1,0:T(8,128)S(1)} %get-tuple-element.113.low), channel_id=1, source_target_pairs={{0,28},{4,0},{8,4},{12,8},{16,12},{20,16},{24,20},{28,24},{1,29},{... | collective-permute-start | bytes 24584 | tf_op jit(solution)/shard_map/ppermute | solution.py:908
  59.5 4.0 %collective-permute-start.14 = (f32[2,8,128]{2,1,0:T(8,128)S(1)}, f32[2,8,128]{2,1,0:T(8,128)S(1)}, u32[]{:S(2)}, u32[]{:S(2)}) collective-permute-start(f32[2,8,128]{2,1,0:T(8,128)S(1)} %get-tuple-element.114.high), channel_id=1, source_target_pairs={{0,4},{4,8},{8,12},{12,16},{16,20},{20,24},{24,28},{28,0},{1,5},{5... | collective-permute-start | bytes 24584 | tf_op jit(solution)/shard_map/ppermute | solution.py:908
  64.7 5.9 %collective-permute-start.16 = (f32[1,128,128]{2,1,0:T(8,128)S(1)}, f32[1,128,128]{2,1,0:T(8,128)S(1)}, u32[]{:S(2)}, u32[]{:S(2)}) collective-permute-start(f32[1,128,128]{2,1,0:T(8,128)S(1)} %get-tuple-element.116), channel_id=1, source_target_pairs={{0,2},{1,3},{2,0},{3,1},{4,6},{5,7},{6,4},{7,5},{8,10},{9,11},{10,... | collective-permute-start | bytes 196616 | tf_op jit(solution)/shard_map/ppermute | solution.py:921
  64.8 5.5 %collective-permute-start.17 = (f32[2,8,128]{2,1,0:T(8,128)S(1)}, f32[2,8,128]{2,1,0:T(8,128)S(1)}, u32[]{:S(2)}, u32[]{:S(2)}) collective-permute-start(f32[2,8,128]{2,1,0:T(8,128)S(1)} %get-tuple-element.118.side), channel_id=1, source_target_pairs={{0,1},{1,2},{2,3},{3,0},{4,5},{5,6},{6,7},{7,4},{8,9},{9,10},{10,1... | collective-permute-start | bytes 24584 | tf_op jit(solution)/shard_map/ppermute | solution.py:908
  70.7 4.3 %collective-permute-start.18 = (f32[128,128]{1,0:T(8,128)S(1)}, f32[128,128]{1,0:T(8,128)S(1)}, u32[]{:S(2)}, u32[]{:S(2)}) collective-permute-start(f32[128,128]{1,0:T(8,128)S(1)} %get-tuple-element.119.x), channel_id=1, source_target_pairs={{0,8},{4,12},{8,0},{12,4},{16,24},{20,28},{24,16},{28,20},{1,9},{5... | collective-permute-start | bytes 196616 | tf_op jit(solution)/shard_map/ppermute | solution.py:921
  71.3 3.7 %collective-permute-start.19 = (f32[2,8,128]{2,1,0:T(8,128)S(1)}, f32[2,8,128]{2,1,0:T(8,128)S(1)}, u32[]{:S(2)}, u32[]{:S(2)}) collective-permute-start(f32[2,8,128]{2,1,0:T(8,128)S(1)} %get-tuple-element.117.side), channel_id=1, source_target_pairs={{0,3},{1,0},{2,1},{3,2},{4,7},{5,4},{6,5},{7,6},{8,11},{9,8},{10,9... | collective-permute-start | bytes 24584 | tf_op jit(solution)/shard_map/ppermute | solution.py:908
  75.0 4.3 %collective-permute-start.20 = (f32[128,128]{1,0:T(8,128)S(1)}, f32[128,128]{1,0:T(8,128)S(1)}, u32[]{:S(2)}, u32[]{:S(2)}) collective-permute-start(f32[128,128]{1,0:T(8,128)S(1)} %get-tuple-element.120.x), channel_id=1, source_target_pairs={{0,16},{4,20},{8,24},{12,28},{16,0},{20,4},{24,8},{28,12},{1,17},{... | collective-permute-start | bytes 196616 | tf_op jit(solution)/shard_map/ppermute | solution.py:921
  79.4 1.3 %collective-permute-start.21 = (f32[128,128]{1,0:T(8,128)S(1)}, f32[128,128]{1,0:T(8,128)S(1)}, u32[]{:S(2)}, u32[]{:S(2)}) collective-permute-start(f32[128,128]{1,0:T(8,128)S(1)} %shard_map.290.mine), channel_id=1, source_target_pairs={{0,4},{4,0},{8,12},{12,8},{16,20},{20,16},{24,28},{28,24},{1,5},{5... | collective-permute-start | bytes 196616 | tf_op jit(solution)/shard_map/ppermute | solution.py:921
where the time goes:
time: 82.1 us; the launch traced here: 81.7 us
  waiting for transfers between devices  40 us (49%)
  starting transfers between devices  16.2 us (20%)
  Pallas kernels  15.1 us (18%)
  blocking collectives  8.9 us (11%)
  between operations  1.42 us (2%)
    ppermute x16, waiting for transfers between devices, shift(): lax.ppermute(x, axis, [(i, (i + step) % count) for i in range(count)])  33.9 us
    pallas_call x17, Pallas kernels, call(): pl.pallas_call(body, out_shape=[(pltpu.VMEM if keep else jax.ShapeDtypeSt...  15.1 us
    ppermute x16, starting transfers between devices, shift(): lax.ppermute(x, axis, [(i, (i + step) % count) for i in range(count)])  13.9 us
    all_to_all x1, blocking collectives, device_step(): lax.all_to_all(hist.reshape(devices, 1, bin_total), ('slab', 'cross'), 0, 0)  8.9 us
    ppermute x6, waiting for transfers between devices, swap(): lax.ppermute(x, axis, [(i, i ^ bit) for i in range(lax.axis_size(axis))])  6.12 us
    ppermute x6, starting transfers between devices, swap(): lax.ppermute(x, axis, [(i, i ^ bit) for i in range(lax.axis_size(axis))])  2.3 us
  transfers between devices with their start and end apart: 22, of which 21 were waited for; matrix products, arithmetic and copies ran while one was open for 0% of the time, Pallas kernels for 5%

commit v1 on v0

--- a/solution.py
+++ b/solution.py
@@ -151,7 +151,7 @@
     return sums[0:16] + (sums[16:32] + sums[32:48])
 
 
-def pool_partials(deltas_bar, code, send_index, outs, scratch, lanes):
+def pool_partials(deltas_bar, code, send_index, outs, groups, scratch, lanes):
     group = code // lanes
     values = []
     for j in range(4):
@@ -164,18 +164,18 @@
     for j in range(4):
         start, width = own_lanes(j, lanes)
         own = jnp.logical_and(place >= start, place < start + width)
-        out_ref = outs[j // 2]
-        out_ref[j % 2, :, :] = jnp.zeros((8, lanes), f32)
+        groups[j, :, :] = jnp.zeros((8, lanes), f32)
         for c in range(3):
             mine = lane_take(jnp.broadcast_to(centres[c], (8, lanes)), jnp.broadcast_to(send_index(j), (8, lanes)))
-            out_ref[j % 2, c : c + 1, :] = sums[4 * j + c : 4 * j + c + 1, :] + jnp.where(
+            groups[j, c : c + 1, :] = sums[4 * j + c : 4 * j + c + 1, :] + jnp.where(
                 own, mine[0:1, :], 0.0
             )
+    by_side(groups[...], *outs)
 
 
 def offer_body(
-    pos, vel, mass, species, send_list, low, high, own_out, send_out,
-    pos_v, vel_v, mass_v, species_v, list_v, semaphores,
+    pos, vel, mass, species, send_list, near, far, own_out, send_out,
+    pos_v, vel_v, mass_v, species_v, list_v, groups, semaphores,
 ):
     fetch((pos, vel, mass, species, send_list), (pos_v, vel_v, mass_v, species_v, list_v), semaphores)
     lanes = pos.shape[1]
@@ -197,19 +197,36 @@
         send_out[j : j + 1, :] = row
         own = jnp.logical_and(place >= start, place < start + width)
         taken = jnp.take_along_axis(own_rows, jnp.broadcast_to(row, (8, lanes)), axis=1)
-        out = (low, high)[j // 2]
-        out[j % 2, :, :] = jnp.where(own, taken, 0.0)
-
-
-def turn_body(low, high, from_down, from_up, left, right):
-    for u, (mine, other) in enumerate(((low, from_down), (high, from_up))):
-        left[u, :, :] = mine[0] + other[0]
-        right[u, :, :] = mine[1] + other[1]
+        groups[j, :, :] = jnp.where(own, taken, 0.0)
+    by_side(groups[...], near, far)
+
+
+def parity(axis):
+    return lax.axis_index(axis) % 2 == 1
+
+
+def by_side(groups, near, far):
+    odd = parity("slab")
+    low, high = groups[0:2], groups[2:4]
+    near[...] = jnp.where(odd, low, high)
+    far[...] = jnp.where(odd, high, low)
+
+
+def turn_body(near, far, from_near, from_far, near_out, far_out):
+    odd = parity("slab")
+    near_sum, far_sum = near[...] + from_near[...], far[...] + from_far[...]
+    low, high = jnp.where(odd, near_sum, far_sum), jnp.where(odd, far_sum, near_sum)
+    odd = parity("cross")
+    for u, part in enumerate((low, high)):
+        near_out[u, :, :] = jnp.where(odd, part[0], part[1])
+        far_out[u, :, :] = jnp.where(odd, part[1], part[0])
 
 
 def whole(pieces, j):
-    right = j % 2
-    return pieces[right][j // 2] + pieces[2 + right][j // 2]
+    u = j // 2
+    near_sum, far_sum = pieces[0][u] + pieces[2][u], pieces[1][u] + pieces[3][u]
+    odd = parity("cross")
+    return jnp.where(odd, far_sum, near_sum) if j % 2 else jnp.where(odd, near_sum, far_sum)
 
 
 class Rows:
@@ -462,12 +479,12 @@
 
 
 def force_body(
-    types, depth, left, right, from_left, from_right, own_rows, index, masks, features, colmat, nh, nl, wh, wl,
-    low, high, pool, save, scratch,
+    types, depth, near, far, from_near, from_far, own_rows, index, masks, features, colmat, nh, nl, wh, wl,
+    near_out, far_out, pool, save, groups, scratch,
 ):
     lanes = own_rows.shape[1]
     for j in range(4):
-        pool[j, :, :] = whole((left, right, from_left, from_right), j)
+        pool[j, :, :] = whole((near, far, from_near, from_far), j)
     slots = index.shape[0] - 8
     feat = features.shape[0]
     rows = saved_rows(feat, types, slots)
@@ -588,7 +605,7 @@
     x_sum = sb[0] + unit[0] * sb[1] + unit[1] * sb[2] + unit[2] * sb[3]
     rb = e * x_sum + e1 * (sa[0] + z_sum) - ir * e * z_sum
     deltas_bar = [rb * unit[c] + e * ir * sa[c + 1] for c in range(3)]
-    pool_partials(deltas_bar, code, lambda j: index[slots + j : slots + j + 1, :], (low, high), scratch, lanes)
+    pool_partials(deltas_bar, code, lambda j: index[slots + j : slots + j + 1, :], (near_out, far_out), groups, scratch, lanes)
 
 
 def centres_of(bins, bin_total):
@@ -596,7 +613,7 @@
 
 
 def hist_body(
-    depth, bin_total, pool, left, right, from_left, from_right, index, masks, bins,
+    depth, bin_total, pool, near, far, from_near, from_far, index, masks, bins,
     next_own, slopes, hist, moved, scratch,
 ):
     lanes = pool.shape[2]
@@ -606,7 +623,7 @@
     mask = masks[0:slots, :]
     for j in range(4):
         kick = (0.5 * time_step * time_step) * pool[j, 6:7, :]
-        force = whole((left, right, from_left, from_right), j)
+        force = whole((near, far, from_near, from_far), j)
         moved[j, 0:3, :] = pool[j, 0:3, :] + time_step * pool[j, 3:6, :] - kick * force[0:3, :]
     inverse8 = jnp.broadcast_to(inverse, (8, lanes))
     own = []
@@ -630,7 +647,7 @@
     hist[...] = jnp.broadcast_to(sums[0:1, :], hist.shape)
 
 
-def adjoint_body(atoms_total, hists, target, slopes, index, bins, low, high, scratch):
+def adjoint_body(atoms_total, hists, target, slopes, index, bins, near, far, groups, scratch):
     lanes = bins.shape[1]
     slots = bins.shape[0]
     code = index[0:slots, :]
@@ -638,11 +655,11 @@
     weights = 2.0 * (total / atoms_total - target[...]) / atoms_total
     picked = lane_take(weights, bins[...])
     deltas_bar = [picked * slopes[c * slots : (c + 1) * slots, :] for c in range(3)]
-    pool_partials(deltas_bar, code, lambda j: index[slots + j : slots + j + 1, :], (low, high), scratch, lanes)
+    pool_partials(deltas_bar, code, lambda j: index[slots + j : slots + j + 1, :], (near, far), groups, scratch, lanes)
 
 
 def grads_body(
-    types, pool, left, right, from_left, from_right, index, save, colmat, phi, filt, nh, nl, wh, wl,
+    types, pool, near, far, from_near, from_far, index, save, colmat, phi, filt, nh, nl, wh, wl,
     keep, send, adjoint, after, tangents, grads,
 ):
     lanes = pool.shape[2]
@@ -658,7 +675,7 @@
         return rows.get(save, name)
 
     for j in range(4):
-        adjoint[j, :, :] = whole((left, right, from_left, from_right), j)
+        adjoint[j, :, :] = whole((near, far, from_near, from_far), j)
     probe = [
         [(0.5 * time_step * time_step) * pool[j, 6:7, :] * adjoint[j, c : c + 1, :] for j in range(4)]
         for c in range(3)
@@ -798,7 +815,7 @@
     after[4 * slots : 4 * slots + feat, :] = ds1b
 
 
-def moves_body(types, index, save, after, wh, wl, low, high, sums, scratch):
+def moves_body(types, index, save, after, wh, wl, near, far, sums, groups, scratch):
     lanes = index.shape[1]
     slots = index.shape[0] - 8
     feat = lanes
@@ -856,11 +873,11 @@
         drb * unit[c] + rb * du[c] + (de * ir + e * dir_) * sa[c + 1] + e * ir * dsa[c + 1]
         for c in range(3)
     ]
-    pool_partials(deltas_bar, code, lambda j: index[slots + j : slots + j + 1, :], (low, high), scratch, lanes)
+    pool_partials(deltas_bar, code, lambda j: index[slots + j : slots + j + 1, :], (near, far), groups, scratch, lanes)
 
 
 def last_body(
-    types, parts, atoms_total, mine, other, adjoint, left, right, index, slope, hidden_t, table_t, spreader, next_own,
+    types, parts, atoms_total, mine, other, adjoint, near, far, index, slope, hidden_t, table_t, spreader, next_own,
     next_out, adj, enc, spr, fil, rot, ref, com, spl, rea, col, total,
 ):
     next_out[...] = next_own[...]
@@ -873,9 +890,12 @@
     feat = lanes
     share = feat // parts
     inverse8 = jnp.broadcast_to(index[slots + 4 : slots + 5, :], (8, lanes))
+    crossed = parity("cross")
+    near_v, far_v = near[...], far[...]
+    second = (jnp.where(crossed, near_v, far_v), jnp.where(crossed, far_v, near_v))
     for c in range(3):
         rows = [
-            atoms_total * (adjoint[j, c : c + 1, :] - (left, right)[j % 2][j // 2, c : c + 1, :]) for j in range(4)
+            atoms_total * (adjoint[j, c : c + 1, :] - second[j % 2][j // 2, c : c + 1, :]) for j in range(4)
         ]
         adj[c : c + 1, :] = from_pool(rows, inverse8, lanes)[0:1, :]
     rot[...] = total[0:share, :]
@@ -903,18 +923,18 @@
             col[...] = col_row[:, part * share : (part + 1) * share]
 
 
-def shift(x, axis, step):
+def neighbours_swap(near, far, axis):
     count = lax.axis_size(axis)
-    return lax.ppermute(x, axis, [(i, (i + step) % count) for i in range(count)])
-
-
-def both_ways(first, second, axis):
-    return shift(first, axis, 1), shift(second, axis, -1)
-
-
-def corner_sum(low, high):
-    left, right = call(turn_body, [(low.shape, f32)] * 2, low, high, *both_ways(high, low, "slab"))
-    return (left, right) + both_ways(right, left, "cross")
+    forward = [(i, (i + 1) % count) for i in range(count)]
+    pairs = [[p for a, b in forward if a % 2 == side for p in ((a, b), (b, a))] for side in (0, 1)]
+    from_far = lax.ppermute(far, axis, pairs[1])
+    from_near = lax.ppermute(near, axis, pairs[0])
+    return from_near, from_far
+
+
+def corner_sum(near, far):
+    near, far = call(turn_body, [(near.shape, f32)] * 2, near, far, *neighbours_swap(near, far, "slab"))
+    return (near, far) + neighbours_swap(near, far, "cross")
 
 
 def swap(x, axis, bit):
@@ -930,15 +950,15 @@
         ref[...] = value.reshape(ref.shape)
 
 
-def halve_hold_body(bit, x, other, low, high, keep, send, low_out, high_out):
+def halve_hold_body(bit, x, other, near, far, keep, send, near_out, far_out):
     halve(bit, x, other, keep, send)
-    low_out[...] = low[...]
-    high_out[...] = high[...]
-
-
-def halve_turn_body(bit, x, other, low, high, from_down, from_up, keep, send, left, right):
+    near_out[...] = near[...]
+    far_out[...] = far[...]
+
+
+def halve_turn_body(bit, x, other, near, far, from_near, from_far, keep, send, near_out, far_out):
     halve(bit, x, other, keep, send)
-    turn_body(low, high, from_down, from_up, left, right)
+    turn_body(near, far, from_near, from_far, near_out, far_out)
 
 
 def add_body(x, other, out):
@@ -950,31 +970,30 @@
     add_body(side, from_side, total)
 
 
-def reduce_all(keep, send, low, high):
+def reduce_all(keep, send, near, far):
     slab_count, cross_count = lax.axis_size("slab"), lax.axis_size("cross")
-    group = (low.shape, f32)
+    group = (near.shape, f32)
     other = swap(send, "slab", 1)
-    bit, step, pieces = 1, 0, None
+    bit, step, received = 1, 0, None
     while bit < cross_count:
         half = ((keep.shape[0] // 2,) + keep.shape[1:], f32)
         if step == 0:
-            keep, send, low, high = call(
-                functools.partial(halve_hold_body, bit), [half, half, group, group], keep, other, low, high
+            keep, send, near, far = call(
+                functools.partial(halve_hold_body, bit), [half, half, group, group], keep, other, near, far
             )
-            from_down, from_up = both_ways(high, low, "slab")
+            received = neighbours_swap(near, far, "slab")
         elif step == 1:
-            keep, send, left, right = call(
+            keep, send, near, far = call(
                 functools.partial(halve_turn_body, bit), [half, half, group, group],
-                keep, other, low, high, from_down, from_up,
+                keep, other, near, far, *received,
             )
-            pieces = (left, right) + both_ways(right, left, "cross")
+            received = neighbours_swap(near, far, "cross")
         else:
             raise NotImplementedError
         other = swap(send, "cross", bit)
         bit, step = 2 * bit, step + 1
     x, other = keep[0], other[0]
-    left, right, from_left, from_right = pieces
-    waiting, sides = [(left, from_left), (right, from_right)], []
+    waiting, sides = [(far, received[1]), (near, received[0])], []
 
     def add(x, other):
         shapes = [(x.shape, f32)]
@@ -992,7 +1011,7 @@
     x = add(x, other)
     while waiting:
         sides += call(add_body, [group], *waiting.pop(0))
-    return x, swap(x, "slab", 1), sides
+    return x, swap(x, "slab", 1), sides[::-1]
 
 
 def device_step(
@@ -1016,13 +1035,13 @@
     group = ((2, 8, lanes), f32)
     pool_shape = ((4, 8, lanes), f32)
     pair_scratch = vm((16 * slots, lanes), f32)
-    low, high, own_rows, send = call(
+    near, far, own_rows, send = call(
         offer_body, [group, group, ((8, lanes), f32), ((8, lanes), i32)],
         *in_hbm(positions, velocities, row(inverse_mass), row(species), send_list),
         specs=[HB] * 5,
         scratch=[
             vm((3, lanes), f32), vm((3, lanes), f32), vm((1, lanes), f32), vm((1, lanes), i32),
-            vm(send_list.shape, i32), dma((5,)),
+            vm(send_list.shape, i32), vm((4, 8, lanes), f32), dma((5,)),
         ],
     )
     colmat, nh, nl, wh, wl, phi, slope, hidden_t, table_t, filt, spreader_in = call(
@@ -1054,15 +1073,15 @@
         specs=[HB] * 4 + [SM] + [VM] * 3,
         scratch=[vm((slots, lanes), i32), vm((1, lanes), i32), dma((4,))],
     )
-    pieces = corner_sum(low, high)
+    pieces = corner_sum(near, far)
     save_rows = saved_rows(feat, types, slots).total
-    low, high, pool, save = call(
+    near, far, pool, save = call(
         functools.partial(force_body, types, depth),
         [group, group, pool_shape, ((save_rows, lanes), f32)],
         *pieces, own_rows, index, masks, features, colmat, nh, nl, wh, wl,
-        scratch=[pair_scratch],
-    )
-    pieces = corner_sum(low, high)
+        scratch=[vm((4, 8, lanes), f32), pair_scratch],
+    )
+    pieces = corner_sum(near, far)
     next_positions, slopes, hist = call(
         functools.partial(hist_body, depth, bin_total),
         [((3, lanes), f32), ((3 * slots, lanes), f32), ((devices, bin_total), f32)],
@@ -1070,12 +1089,12 @@
         scratch=[vm((4, 8, lanes), f32), pair_scratch],
     )
     hists = lax.all_to_all(hist.reshape(devices, 1, bin_total), ("slab", "cross"), 0, 0)
-    low, high = call(
+    near, far = call(
         functools.partial(adjoint_body, atoms_total), [group, group],
         hists.reshape(devices, bin_total), goal, slopes, index, bins,
-        scratch=[pair_scratch],
-    )
-    pieces = corner_sum(low, high)
+        scratch=[vm((4, 8, lanes), f32), pair_scratch],
+    )
+    pieces = corner_sum(near, far)
     half_grads = ((parts, feat, lanes), f32)
     keep, send, adjoint, after = call(
         functools.partial(grads_body, types),
@@ -1083,11 +1102,11 @@
         pool, *pieces, index, save, colmat, phi, filt, nh, nl, wh, wl,
         scratch=[vm((4 * STRIDE * types, lanes), f32), vm((parts, 2 * feat, lanes), f32)],
     )
-    low, high = call(
+    near, far = call(
         functools.partial(moves_body, types), [group, group], index, save, after, wh, wl,
-        scratch=[vm((8 * slots, lanes), f32), pair_scratch],
-    )
-    mine, other, sides = reduce_all(keep, send, low, high)
+        scratch=[vm((8 * slots, lanes), f32), vm((4, 8, lanes), f32), pair_scratch],
+    )
+    mine, other, sides = reduce_all(keep, send, near, far)
     share = feat // parts
     results = call(
         functools.partial(last_body, types, parts, atoms_total),

time: 82.1 us -> 78.7 us (0.959)
  waiting for transfers between devices: 40 us -> 32.5 us
  starting transfers between devices: 16.2 us -> 19.7 us
    ppermute x16, waiting for transfers between devices: 33.9 us -> 25.3 us  [the longest x8 17.3 us: neighbours_swap(): from_far = lax.ppermute(far, axis, pairs[1])]
    ppermute x16, starting transfers between devices: 13.9 us -> 18.2 us  [the longest x8 13.7 us: neighbours_swap(): from_far = lax.ppermute(far, axis, pairs[1])]
    ppermute x6, waiting for transfers between devices: 6.12 us -> 7.12 us  [swap(): lax.ppermute(x, axis, [(i, i ^ bit) for i in range(lax.axis_size(axis))])]
    ppermute x6, starting transfers between devices: 2.3 us -> 1.47 us  [swap(): lax.ppermute(x, axis, [(i, i ^ bit) for i in range(lax.axis_size(axis))])]
  transfers between devices with their start and end apart: 22 -> 22, of which waited for: 21 -> 17; matrix products, arithmetic and copies ran while one was open for 0% -> 0% of each run, Pallas kernels for 5% -> 5%
where the time goes in v1:
time: 78.7 us; the launch traced here: 78.4 us
  waiting for transfers between devices  32.5 us (41%)
  starting transfers between devices  19.7 us (25%)
  Pallas kernels  15.2 us (19%)
  blocking collectives  9.55 us (12%)
  between operations  1.44 us (2%)
    ppermute x8, waiting for transfers between devices, neighbours_swap(): from_far = lax.ppermute(far, axis, pairs[1])  17.3 us
    pallas_call x17, Pallas kernels, call(): pl.pallas_call(body, out_shape=[(pltpu.VMEM if keep else jax.ShapeDtypeSt...  15.2 us
    ppermute x8, starting transfers between devices, neighbours_swap(): from_far = lax.ppermute(far, axis, pairs[1])  13.7 us
    all_to_all x1, blocking collectives, device_step(): lax.all_to_all(hist.reshape(devices, 1, bin_total), ('slab', 'cross'), 0, 0)  9.55 us
    ppermute x8, waiting for transfers between devices, neighbours_swap(): from_near = lax.ppermute(near, axis, pairs[0])  8.05 us
    ppermute x6, waiting for transfers between devices, swap(): lax.ppermute(x, axis, [(i, i ^ bit) for i in range(lax.axis_size(axis))])  7.12 us
    ppermute x8, starting transfers between devices, neighbours_swap(): from_near = lax.ppermute(near, axis, pairs[0])  4.52 us
  transfers between devices with their start and end apart: 22, of which 17 were waited for; matrix products, arithmetic and copies ran while one was open for 0% of the time, Pallas kernels for 5%

profile of v1, /device:TPU:0, one launch (start us, length us, event | category | flops | bytes accessed | tf_op | source)
XLA Modules:
  0.0 78.4 jit_solution(54893738816514275)
XLA Ops:
  2.2 3.5 %collective-permute-start.1 = (f32[2,8,128]{2,1,0:T(8,128)S(1)}, f32[2,8,128]{2,1,0:T(8,128)S(1)}, u32[]{:S(2)}, u32[]{:S(2)}) collective-permute-start(f32[2,8,128]{2,1,0:T(8,128)S(1)} %get-tuple-element.76.far), channel_id=1, source_target_pairs={{4,8},{8,4},{12,16},{16,12},{20,24},{24,20},{28,0},{0,28},{5,9},{9... | collective-permute-start | bytes 24584 | tf_op jit(solution)/shard_map/ppermute | solution.py:930
  5.7 1.4 %collective-permute-done.1.from_far = f32[2,8,128]{2,1,0:T(8,128)S(1)} collective-permute-done((f32[2,8,128]{2,1,0:T(8,128)S(1)}, f32[2,8,128]{2,1,0:T(8,128)S(1)}, u32[]{:S(2)}, u32[]{:S(2)}) %collective-permute-start.1) | collective-permute-done | bytes 8224 | tf_op jit(solution)/shard_map/ppermute | solution.py:930
  7.1 1.8 %collective-permute-start.2 = (f32[2,8,128]{2,1,0:T(8,128)S(1)}, f32[2,8,128]{2,1,0:T(8,128)S(1)}, u32[]{:S(2)}, u32[]{:S(2)}) collective-permute-start(f32[2,8,128]{2,1,0:T(8,128)S(1)} %get-tuple-element.77.near), channel_id=1, source_target_pairs={{0,1},{1,0},{2,3},{3,2},{4,5},{5,4},{6,7},{7,6},{8,9},{9,8},{10,11... | collective-permute-start | bytes 24584 | tf_op jit(solution)/shard_map/ppermute | solution.py:931
  8.8 2.5 %collective-permute-start.3 = (f32[2,8,128]{2,1,0:T(8,128)S(1)}, f32[2,8,128]{2,1,0:T(8,128)S(1)}, u32[]{:S(2)}, u32[]{:S(2)}) collective-permute-start(f32[2,8,128]{2,1,0:T(8,128)S(1)} %get-tuple-element.78.far), channel_id=1, source_target_pairs={{1,2},{2,1},{3,0},{0,3},{5,6},{6,5},{7,4},{4,7},{9,10},{10,9},{11,... | collective-permute-start | bytes 24584 | tf_op jit(solution)/shard_map/ppermute | solution.py:930
  12.0 1.9 %shard_map.277 = (f32[128,128]{1,0:T(8,128)S(1)}, bf16[1024,128]{1,0:T(8,128)(2,1)S(1)}, bf16[1024,128]{1,0:T(8,128)(2,1)S(1)}, bf16[896,256]{1,0:T(8,128)(2,1)S...) custom-call(f32[8,128]{1,0:T(8,128)} %table_h.1, ...), custom_call_target="tpu_custom_call" | custom-call | tf_op jit(solution)/shard_map/pallas_call | solution.py:31
  14.9 4.1 %shard_map.279 = (f32[2,8,128]{2,1,0:T(8,128)S(1)}, f32[2,8,128]{2,1,0:T(8,128)S(1)}, f32[4,8,128]{2,1,0:T(8,128)S(1)}, f32[8000,128]{1,0:T(8,128)S(1)}) custom-call(f32[2,8,128]{2,1,0:T(8,128)S(1)} %get-tuple-element.77.near, f32[2,8,128]{2,1,0:T(8,128)S(1)} %get-tuple-element.78.far, f32[2,8,128]{2,1,0:T(8,128)S(1)} %collective-permute-done.2.from_near, ...), custom_call_target="tpu_custom_call" | custom-call | tf_op jit(solution)/shard_map/pallas_call | solution.py:31
  19.1 2.0 %collective-permute-start.5 = (f32[2,8,128]{2,1,0:T(8,128)S(1)}, f32[2,8,128]{2,1,0:T(8,128)S(1)}, u32[]{:S(2)}, u32[]{:S(2)}) collective-permute-start(f32[2,8,128]{2,1,0:T(8,128)S(1)} %get-tuple-element.92.far), channel_id=1, source_target_pairs={{4,8},{8,4},{12,16},{16,12},{20,24},{24,20},{28,0},{0,28},{5,9},{9... | collective-permute-start | bytes 24584 | tf_op jit(solution)/shard_map/ppermute | solution.py:930
  21.0 2.1 %collective-permute-done.5.from_far = f32[2,8,128]{2,1,0:T(8,128)S(1)} collective-permute-done((f32[2,8,128]{2,1,0:T(8,128)S(1)}, f32[2,8,128]{2,1,0:T(8,128)S(1)}, u32[]{:S(2)}, u32[]{:S(2)}) %collective-permute-start.5) | collective-permute-done | bytes 8224 | tf_op jit(solution)/shard_map/ppermute | solution.py:930
  23.8 1.2 %collective-permute-start.7 = (f32[2,8,128]{2,1,0:T(8,128)S(1)}, f32[2,8,128]{2,1,0:T(8,128)S(1)}, u32[]{:S(2)}, u32[]{:S(2)}) collective-permute-start(f32[2,8,128]{2,1,0:T(8,128)S(1)} %get-tuple-element.94.far), channel_id=1, source_target_pairs={{1,2},{2,1},{3,0},{0,3},{5,6},{6,5},{7,4},{4,7},{9,10},{10,9},{11,... | collective-permute-start | bytes 24584 | tf_op jit(solution)/shard_map/ppermute | solution.py:930
  25.1 1.8 %collective-permute-done.6.from_near = f32[2,8,128]{2,1,0:T(8,128)S(1)} collective-permute-done((f32[2,8,128]{2,1,0:T(8,128)S(1)}, f32[2,8,128]{2,1,0:T(8,128)S(1)}, u32[]{:S(2)}, u32[]{:S(2)}) %collective-permute-start.6) | collective-permute-done | bytes 8224 | tf_op jit(solution)/shard_map/ppermute | solution.py:931
  26.8 2.5 %collective-permute-done.7.from_far = f32[2,8,128]{2,1,0:T(8,128)S(1)} collective-permute-done((f32[2,8,128]{2,1,0:T(8,128)S(1)}, f32[2,8,128]{2,1,0:T(8,128)S(1)}, u32[]{:S(2)}, u32[]{:S(2)}) %collective-permute-start.7) | collective-permute-done | bytes 8224 | tf_op jit(solution)/shard_map/ppermute | solution.py:930
  29.7 9.6 %all_to_all.5 = f32[32,1,128]{2,1,0:T(1,128)S(1)} all-to-all(f32[32,1,128]{2,1,0:T(1,128)S(1)} %bitcast.17), channel_id=1, replica_groups=mesh['slab'=8,'cross'=4] {'slab','cross'}, dimensions={0} | all-to-all | bytes 32768 | tf_op jit(solution)/shard_map/all_to_all | solution.py:1091
  40.9 2.9 %collective-permute-done.9.from_far = f32[2,8,128]{2,1,0:T(8,128)S(1)} collective-permute-done((f32[2,8,128]{2,1,0:T(8,128)S(1)}, f32[2,8,128]{2,1,0:T(8,128)S(1)}, u32[]{:S(2)}, u32[]{:S(2)}) %collective-permute-start.9) | collective-permute-done | bytes 8224 | tf_op jit(solution)/shard_map/ppermute | solution.py:930
  44.3 1.5 %collective-permute-start.11 = (f32[2,8,128]{2,1,0:T(8,128)S(1)}, f32[2,8,128]{2,1,0:T(8,128)S(1)}, u32[]{:S(2)}, u32[]{:S(2)}) collective-permute-start(f32[2,8,128]{2,1,0:T(8,128)S(1)} %get-tuple-element.102.far), channel_id=1, source_target_pairs={{1,2},{2,1},{3,0},{0,3},{5,6},{6,5},{7,4},{4,7},{9,10},{10,9},{11,... | collective-permute-start | bytes 24584 | tf_op jit(solution)/shard_map/ppermute | solution.py:930
  45.8 1.7 %collective-permute-done.10.from_near = f32[2,8,128]{2,1,0:T(8,128)S(1)} collective-permute-done((f32[2,8,128]{2,1,0:T(8,128)S(1)}, f32[2,8,128]{2,1,0:T(8,128)S(1)}, u32[]{:S(2)}, u32[]{:S(2)}) %collective-permute-start.10) | collective-permute-done | bytes 8224 | tf_op jit(solution)/shard_map/ppermute | solution.py:931
  47.5 2.3 %collective-permute-done.11.from_far = f32[2,8,128]{2,1,0:T(8,128)S(1)} collective-permute-done((f32[2,8,128]{2,1,0:T(8,128)S(1)}, f32[2,8,128]{2,1,0:T(8,128)S(1)}, u32[]{:S(2)}, u32[]{:S(2)}) %collective-permute-start.11) | collective-permute-done | bytes 8224 | tf_op jit(solution)/shard_map/ppermute | solution.py:930
  49.8 4.1 %shard_map.284 = (f32[4,128,128]{2,1,0:T(8,128)S(1)}, f32[4,128,128]{2,1,0:T(8,128)S(1)}, f32[4,8,128]{2,1,0:T(8,128)S(1)}, f32[576,128]{1,0:T(8,128)S(1)}) custom-call(f32[4,8,128]{2,1,0:T(8,128)S(1)} %get-tuple-element.90.pool, f32[2,8,128]{2,1,0:T(8,128)S(1)} %get-tuple-element.101.near, f32[2,8,128]{2,1,0:T(8,128)S(1)} %get-tuple-element.102.far, ...), custom_call_target="tpu_custom_call" | custom-call | tf_op jit(solution)/shard_map/pallas_call | solution.py:31
  56.8 3.0 %collective-permute-done.15.from_far = f32[2,8,128]{2,1,0:T(8,128)S(1)} collective-permute-done((f32[2,8,128]{2,1,0:T(8,128)S(1)}, f32[2,8,128]{2,1,0:T(8,128)S(1)}, u32[]{:S(2)}, u32[]{:S(2)}) %collective-permute-start.15) | collective-permute-done | bytes 8224 | tf_op jit(solution)/shard_map/ppermute | solution.py:930
  59.9 1.3 %collective-permute-done.13.other = f32[2,128,128]{2,1,0:T(8,128)S(1)} collective-permute-done((f32[2,128,128]{2,1,0:T(8,128)S(1)}, f32[2,128,128]{2,1,0:T(8,128)S(1)}, u32[]{:S(2)}, u32[]{:S(2)}) %collective-permute-start.13) | collective-permute-done | bytes 131104 | tf_op jit(solution)/shard_map/ppermute | solution.py:941
  61.7 2.3 %collective-permute-start.17 = (f32[2,8,128]{2,1,0:T(8,128)S(1)}, f32[2,8,128]{2,1,0:T(8,128)S(1)}, u32[]{:S(2)}, u32[]{:S(2)}) collective-permute-start(f32[2,8,128]{2,1,0:T(8,128)S(1)} %get-tuple-element.117.side), channel_id=1, source_target_pairs={{1,2},{2,1},{3,0},{0,3},{5,6},{6,5},{7,4},{4,7},{9,10},{10,9},{11,... | collective-permute-start | bytes 24584 | tf_op jit(solution)/shard_map/ppermute | solution.py:930
  64.1 3.2 %collective-permute-done.17.from_side = f32[2,8,128]{2,1,0:T(8,128)S(1)} collective-permute-done((f32[2,8,128]{2,1,0:T(8,128)S(1)}, f32[2,8,128]{2,1,0:T(8,128)S(1)}, u32[]{:S(2)}, u32[]{:S(2)}) %collective-permute-start.17) | collective-permute-done | bytes 8224 | tf_op jit(solution)/shard_map/ppermute | solution.py:930
  67.9 3.2 %collective-permute-done.19.from_side = f32[2,8,128]{2,1,0:T(8,128)S(1)} collective-permute-done((f32[2,8,128]{2,1,0:T(8,128)S(1)}, f32[2,8,128]{2,1,0:T(8,128)S(1)}, u32[]{:S(2)}, u32[]{:S(2)}) %collective-permute-start.19) | collective-permute-done | bytes 8224 | tf_op jit(solution)/shard_map/ppermute | solution.py:931
  72.3 3.7 %collective-permute-done.20.other = f32[128,128]{1,0:T(8,128)S(1)} collective-permute-done((f32[128,128]{1,0:T(8,128)S(1)}, f32[128,128]{1,0:T(8,128)S(1)}, u32[]{:S(2)}, u32[]{:S(2)}) %collective-permute-start.20) | collective-permute-done | bytes 65568 | tf_op jit(solution)/shard_map/ppermute | solution.py:941
  76.1 1.2 %collective-permute-done.21.other = f32[128,128]{1,0:T(8,128)S(1)} collective-permute-done((f32[128,128]{1,0:T(8,128)S(1)}, f32[128,128]{1,0:T(8,128)S(1)}, u32[]{:S(2)}, u32[]{:S(2)}) %collective-permute-start.21) | collective-permute-done | bytes 65568 | tf_op jit(solution)/shard_map/ppermute | solution.py:941
  (38 shorter events, 12.3 us)
Async XLA Ops:
  1.6 4.1 %collective-permute-start = (f32[2,8,128]{2,1,0:T(8,128)S(1)}, f32[2,8,128]{2,1,0:T(8,128)S(1)}, u32[]{:S(2)}, u32[]{:S(2)}) collective-permute-start(f32[2,8,128]{2,1,0:T(8,128)S(1)} %get-tuple-element.75.near), channel_id=1, source_target_pairs={{0,4},{4,0},{8,12},{12,8},{16,20},{20,16},{24,28},{28,24},{1,5},{5... | collective-permute-start | bytes 24584 | tf_op jit(solution)/shard_map/ppermute | solution.py:931
  2.2 4.9 %collective-permute-start.1 = (f32[2,8,128]{2,1,0:T(8,128)S(1)}, f32[2,8,128]{2,1,0:T(8,128)S(1)}, u32[]{:S(2)}, u32[]{:S(2)}) collective-permute-start(f32[2,8,128]{2,1,0:T(8,128)S(1)} %get-tuple-element.76.far), channel_id=1, source_target_pairs={{4,8},{8,4},{12,16},{16,12},{20,24},{24,20},{28,0},{0,28},{5,9},{9... | collective-permute-start | bytes 24584 | tf_op jit(solution)/shard_map/ppermute | solution.py:930
  7.1 7.8 %collective-permute-start.2 = (f32[2,8,128]{2,1,0:T(8,128)S(1)}, f32[2,8,128]{2,1,0:T(8,128)S(1)}, u32[]{:S(2)}, u32[]{:S(2)}) collective-permute-start(f32[2,8,128]{2,1,0:T(8,128)S(1)} %get-tuple-element.77.near), channel_id=1, source_target_pairs={{0,1},{1,0},{2,3},{3,2},{4,5},{5,4},{6,7},{7,6},{8,9},{9,8},{10,11... | collective-permute-start | bytes 24584 | tf_op jit(solution)/shard_map/ppermute | solution.py:931
  8.8 6.1 %collective-permute-start.3 = (f32[2,8,128]{2,1,0:T(8,128)S(1)}, f32[2,8,128]{2,1,0:T(8,128)S(1)}, u32[]{:S(2)}, u32[]{:S(2)}) collective-permute-start(f32[2,8,128]{2,1,0:T(8,128)S(1)} %get-tuple-element.78.far), channel_id=1, source_target_pairs={{1,2},{2,1},{3,0},{0,3},{5,6},{6,5},{7,4},{4,7},{9,10},{10,9},{11,... | collective-permute-start | bytes 24584 | tf_op jit(solution)/shard_map/ppermute | solution.py:930
  19.0 2.0 %collective-permute-start.4 = (f32[2,8,128]{2,1,0:T(8,128)S(1)}, f32[2,8,128]{2,1,0:T(8,128)S(1)}, u32[]{:S(2)}, u32[]{:S(2)}) collective-permute-start(f32[2,8,128]{2,1,0:T(8,128)S(1)} %get-tuple-element.91.near), channel_id=1, source_target_pairs={{0,4},{4,0},{8,12},{12,8},{16,20},{20,16},{24,28},{28,24},{1,5},{5... | collective-permute-start | bytes 24584 | tf_op jit(solution)/shard_map/ppermute | solution.py:931
  19.1 4.0 %collective-permute-start.5 = (f32[2,8,128]{2,1,0:T(8,128)S(1)}, f32[2,8,128]{2,1,0:T(8,128)S(1)}, u32[]{:S(2)}, u32[]{:S(2)}) collective-permute-start(f32[2,8,128]{2,1,0:T(8,128)S(1)} %get-tuple-element.92.far), channel_id=1, source_target_pairs={{4,8},{8,4},{12,16},{16,12},{20,24},{24,20},{28,0},{0,28},{5,9},{9... | collective-permute-start | bytes 24584 | tf_op jit(solution)/shard_map/ppermute | solution.py:930
  23.1 3.7 %collective-permute-start.6 = (f32[2,8,128]{2,1,0:T(8,128)S(1)}, f32[2,8,128]{2,1,0:T(8,128)S(1)}, u32[]{:S(2)}, u32[]{:S(2)}) collective-permute-start(f32[2,8,128]{2,1,0:T(8,128)S(1)} %get-tuple-element.93.near), channel_id=1, source_target_pairs={{0,1},{1,0},{2,3},{3,2},{4,5},{5,4},{6,7},{7,6},{8,9},{9,8},{10,11... | collective-permute-start | bytes 24584 | tf_op jit(solution)/shard_map/ppermute | solution.py:931
  23.8 5.4 %collective-permute-start.7 = (f32[2,8,128]{2,1,0:T(8,128)S(1)}, f32[2,8,128]{2,1,0:T(8,128)S(1)}, u32[]{:S(2)}, u32[]{:S(2)}) collective-permute-start(f32[2,8,128]{2,1,0:T(8,128)S(1)} %get-tuple-element.94.far), channel_id=1, source_target_pairs={{1,2},{2,1},{3,0},{0,3},{5,6},{6,5},{7,4},{4,7},{9,10},{10,9},{11,... | collective-permute-start | bytes 24584 | tf_op jit(solution)/shard_map/ppermute | solution.py:930
  39.6 1.2 %collective-permute-start.8 = (f32[2,8,128]{2,1,0:T(8,128)S(1)}, f32[2,8,128]{2,1,0:T(8,128)S(1)}, u32[]{:S(2)}, u32[]{:S(2)}) collective-permute-start(f32[2,8,128]{2,1,0:T(8,128)S(1)} %get-tuple-element.99.near), channel_id=1, source_target_pairs={{0,4},{4,0},{8,12},{12,8},{16,20},{20,16},{24,28},{28,24},{1,5},{5... | collective-permute-start | bytes 24584 | tf_op jit(solution)/shard_map/ppermute | solution.py:931
  39.7 4.0 %collective-permute-start.9 = (f32[2,8,128]{2,1,0:T(8,128)S(1)}, f32[2,8,128]{2,1,0:T(8,128)S(1)}, u32[]{:S(2)}, u32[]{:S(2)}) collective-permute-start(f32[2,8,128]{2,1,0:T(8,128)S(1)} %get-tuple-element.100.far), channel_id=1, source_target_pairs={{4,8},{8,4},{12,16},{16,12},{20,24},{24,20},{28,0},{0,28},{5,9},{9... | collective-permute-start | bytes 24584 | tf_op jit(solution)/shard_map/ppermute | solution.py:930
  43.8 3.7 %collective-permute-start.10 = (f32[2,8,128]{2,1,0:T(8,128)S(1)}, f32[2,8,128]{2,1,0:T(8,128)S(1)}, u32[]{:S(2)}, u32[]{:S(2)}) collective-permute-start(f32[2,8,128]{2,1,0:T(8,128)S(1)} %get-tuple-element.101.near), channel_id=1, source_target_pairs={{0,1},{1,0},{2,3},{3,2},{4,5},{5,4},{6,7},{7,6},{8,9},{9,8},{10,11... | collective-permute-start | bytes 24584 | tf_op jit(solution)/shard_map/ppermute | solution.py:931
  44.3 5.4 %collective-permute-start.11 = (f32[2,8,128]{2,1,0:T(8,128)S(1)}, f32[2,8,128]{2,1,0:T(8,128)S(1)}, u32[]{:S(2)}, u32[]{:S(2)}) collective-permute-start(f32[2,8,128]{2,1,0:T(8,128)S(1)} %get-tuple-element.102.far), channel_id=1, source_target_pairs={{1,2},{2,1},{3,0},{0,3},{5,6},{6,5},{7,4},{4,7},{9,10},{10,9},{11,... | collective-permute-start | bytes 24584 | tf_op jit(solution)/shard_map/ppermute | solution.py:930
  53.9 1.6 %collective-permute-start.12 = (f32[4,128,128]{2,1,0:T(8,128)S(1)}, f32[4,128,128]{2,1,0:T(8,128)S(1)}, u32[]{:S(2)}, u32[]{:S(2)}) collective-permute-start(f32[4,128,128]{2,1,0:T(8,128)S(1)} %get-tuple-element.107), channel_id=1, source_target_pairs={{0,4},{4,0},{8,12},{12,8},{16,20},{20,16},{24,28},{28,24},{1,5},{5... | collective-permute-start | bytes 786440 | tf_op jit(solution)/shard_map/ppermute | solution.py:941
  55.5 5.7 %collective-permute-start.13 = (f32[2,128,128]{2,1,0:T(8,128)S(1)}, f32[2,128,128]{2,1,0:T(8,128)S(1)}, u32[]{:S(2)}, u32[]{:S(2)}) collective-permute-start(f32[2,128,128]{2,1,0:T(8,128)S(1)} %get-tuple-element.112), channel_id=1, source_target_pairs={{0,1},{1,0},{2,3},{3,2},{4,5},{5,4},{6,7},{7,6},{8,9},{9,8},{10,11... | collective-permute-start | bytes 393224 | tf_op jit(solution)/shard_map/ppermute | solution.py:941
  55.6 1.2 %collective-permute-start.14 = (f32[2,8,128]{2,1,0:T(8,128)S(1)}, f32[2,8,128]{2,1,0:T(8,128)S(1)}, u32[]{:S(2)}, u32[]{:S(2)}) collective-permute-start(f32[2,8,128]{2,1,0:T(8,128)S(1)} %get-tuple-element.113.near), channel_id=1, source_target_pairs={{0,4},{4,0},{8,12},{12,8},{16,20},{20,16},{24,28},{28,24},{1,5},{5... | collective-permute-start | bytes 24584 | tf_op jit(solution)/shard_map/ppermute | solution.py:931
  55.9 4.0 %collective-permute-start.15 = (f32[2,8,128]{2,1,0:T(8,128)S(1)}, f32[2,8,128]{2,1,0:T(8,128)S(1)}, u32[]{:S(2)}, u32[]{:S(2)}) collective-permute-start(f32[2,8,128]{2,1,0:T(8,128)S(1)} %get-tuple-element.114.far), channel_id=1, source_target_pairs={{4,8},{8,4},{12,16},{16,12},{20,24},{24,20},{28,0},{0,28},{5,9},{9... | collective-permute-start | bytes 24584 | tf_op jit(solution)/shard_map/ppermute | solution.py:930
  61.2 6.1 %collective-permute-start.16 = (f32[1,128,128]{2,1,0:T(8,128)S(1)}, f32[1,128,128]{2,1,0:T(8,128)S(1)}, u32[]{:S(2)}, u32[]{:S(2)}) collective-permute-start(f32[1,128,128]{2,1,0:T(8,128)S(1)} %get-tuple-element.116), channel_id=1, source_target_pairs={{0,2},{1,3},{2,0},{3,1},{4,6},{5,7},{6,4},{7,5},{8,10},{9,11},{10,... | collective-permute-start | bytes 196616 | tf_op jit(solution)/shard_map/ppermute | solution.py:941
  61.7 5.5 %collective-permute-start.17 = (f32[2,8,128]{2,1,0:T(8,128)S(1)}, f32[2,8,128]{2,1,0:T(8,128)S(1)}, u32[]{:S(2)}, u32[]{:S(2)}) collective-permute-start(f32[2,8,128]{2,1,0:T(8,128)S(1)} %get-tuple-element.117.side), channel_id=1, source_target_pairs={{1,2},{2,1},{3,0},{0,3},{5,6},{6,5},{7,4},{4,7},{9,10},{10,9},{11,... | collective-permute-start | bytes 24584 | tf_op jit(solution)/shard_map/ppermute | solution.py:930
  67.3 4.3 %collective-permute-start.18 = (f32[128,128]{1,0:T(8,128)S(1)}, f32[128,128]{1,0:T(8,128)S(1)}, u32[]{:S(2)}, u32[]{:S(2)}) collective-permute-start(f32[128,128]{1,0:T(8,128)S(1)} %get-tuple-element.118.x), channel_id=1, source_target_pairs={{0,8},{4,12},{8,0},{12,4},{16,24},{20,28},{24,16},{28,20},{1,9},{5... | collective-permute-start | bytes 196616 | tf_op jit(solution)/shard_map/ppermute | solution.py:941
  67.4 3.7 %collective-permute-start.19 = (f32[2,8,128]{2,1,0:T(8,128)S(1)}, f32[2,8,128]{2,1,0:T(8,128)S(1)}, u32[]{:S(2)}, u32[]{:S(2)}) collective-permute-start(f32[2,8,128]{2,1,0:T(8,128)S(1)} %get-tuple-element.119.side), channel_id=1, source_target_pairs={{0,1},{1,0},{2,3},{3,2},{4,5},{5,4},{6,7},{7,6},{8,9},{9,8},{10,11... | collective-permute-start | bytes 24584 | tf_op jit(solution)/shard_map/ppermute | solution.py:931
  71.6 4.3 %collective-permute-start.20 = (f32[128,128]{1,0:T(8,128)S(1)}, f32[128,128]{1,0:T(8,128)S(1)}, u32[]{:S(2)}, u32[]{:S(2)}) collective-permute-start(f32[128,128]{1,0:T(8,128)S(1)} %get-tuple-element.120.x), channel_id=1, source_target_pairs={{0,16},{4,20},{8,24},{12,28},{16,0},{20,4},{24,8},{28,12},{1,17},{... | collective-permute-start | bytes 196616 | tf_op jit(solution)/shard_map/ppermute | solution.py:941
  76.0 1.3 %collective-permute-start.21 = (f32[128,128]{1,0:T(8,128)S(1)}, f32[128,128]{1,0:T(8,128)S(1)}, u32[]{:S(2)}, u32[]{:S(2)}) collective-permute-start(f32[128,128]{1,0:T(8,128)S(1)} %shard_map.290.mine), channel_id=1, source_target_pairs={{0,4},{4,0},{8,12},{12,8},{16,20},{20,16},{24,28},{28,24},{1,5},{5... | collective-permute-start | bytes 196616 | tf_op jit(solution)/shard_map/ppermute | solution.py:941

commit v2 on v1

--- a/solution.py
+++ b/solution.py
@@ -965,9 +965,17 @@
     out[...] = x[...] + other[...]
 
 
-def add_two_body(x, other, side, from_side, out, total):
+def add_sides_body(x, other, near, far, from_near, from_far, out, near_out, far_out):
     add_body(x, other, out)
-    add_body(side, from_side, total)
+    add_body(near, from_near, near_out)
+    add_body(far, from_far, far_out)
+
+
+def add_all_body(*refs):
+    total = refs[0][...]
+    for ref in refs[1:-1]:
+        total = total + ref[...]
+    refs[-1][...] = total
 
 
 def reduce_all(keep, send, near, far):
@@ -993,25 +1001,13 @@
         other = swap(send, "cross", bit)
         bit, step = 2 * bit, step + 1
     x, other = keep[0], other[0]
-    waiting, sides = [(far, received[1]), (near, received[0])], []
-
-    def add(x, other):
-        shapes = [(x.shape, f32)]
-        if waiting:
-            x, side = call(add_two_body, shapes + [group], x, other, *waiting.pop(0))
-            sides.append(side)
-            return x
-        return call(add_body, shapes, x, other)[0]
-
-    bit = 2
-    while bit < slab_count:
-        x = add(x, other)
-        other = swap(x, "slab", bit)
-        bit *= 2
-    x = add(x, other)
-    while waiting:
-        sides += call(add_body, [group], *waiting.pop(0))
-    return x, swap(x, "slab", 1), sides[::-1]
+    x, *sides = call(add_sides_body, [(x.shape, f32), group, group], x, other, near, far, *received)
+    bits = [2**b for b in range(1, slab_count.bit_length()) if 2**b < slab_count]
+    for i in range(0, len(bits), 2):
+        pair = bits[i : i + 2]
+        steps = pair + [sum(pair)] * (len(pair) - 1)
+        (x,) = call(add_all_body, [(x.shape, f32)], x, *[swap(x, "slab", step) for step in steps])
+    return x, swap(x, "slab", 1), sides
 
 
 def device_step(

time: 78.7 us -> 77.4 us (0.983)
  waiting for transfers between devices: 32.5 us -> 27.3 us
  starting transfers between devices: 19.7 us -> 23.6 us
    ppermute x8, waiting for transfers between devices: 8.05 us -> 4.89 us  [neighbours_swap(): from_near = lax.ppermute(near, axis, pairs[0])]
    ppermute x6 -> x7, starting transfers between devices: 1.47 us -> 4.28 us  [swap(): lax.ppermute(x, axis, [(i, i ^ bit) for i in range(lax.axis_size(axis))])]
    ppermute x6 -> x7, waiting for transfers between devices: 7.12 us -> 5.16 us  [swap(): lax.ppermute(x, axis, [(i, i ^ bit) for i in range(lax.axis_size(axis))])]
    ppermute x8, starting transfers between devices: 4.52 us -> 5.58 us  [neighbours_swap(): from_near = lax.ppermute(near, axis, pairs[0])]
    pallas_call x17 -> x16, Pallas kernels: 15.2 us -> 15.2 us  [call(): pl.pallas_call(body, out_shape=[(pltpu.VMEM if keep else jax.ShapeDtypeSt...]
  transfers between devices with their start and end apart: 22 -> 23, of which waited for: 17 -> 16; matrix products, arithmetic and copies ran while one was open for 0% -> 0% of each run, Pallas kernels for 5% -> 5%
where the time goes in v2:
time: 77.4 us; the launch traced here: 77 us
  waiting for transfers between devices  27.3 us (35%)
  starting transfers between devices  23.6 us (30%)
  Pallas kernels  15.2 us (20%)
  blocking collectives  9.55 us (12%)
  between operations  1.44 us (2%)
    ppermute x8, waiting for transfers between devices, neighbours_swap(): from_far = lax.ppermute(far, axis, pairs[1])  17.2 us
    pallas_call x16, Pallas kernels, call(): pl.pallas_call(body, out_shape=[(pltpu.VMEM if keep else jax.ShapeDtypeSt...  15.2 us
    ppermute x8, starting transfers between devices, neighbours_swap(): from_far = lax.ppermute(far, axis, pairs[1])  13.7 us
    all_to_all x1, blocking collectives, device_step(): lax.all_to_all(hist.reshape(devices, 1, bin_total), ('slab', 'cross'), 0, 0)  9.55 us
    ppermute x8, starting transfers between devices, neighbours_swap(): from_near = lax.ppermute(near, axis, pairs[0])  5.58 us
    ppermute x7, waiting for transfers between devices, swap(): lax.ppermute(x, axis, [(i, i ^ bit) for i in range(lax.axis_size(axis))])  5.16 us
    ppermute x8, waiting for transfers between devices, neighbours_swap(): from_near = lax.ppermute(near, axis, pairs[0])  4.89 us
    ppermute x7, starting transfers between devices, swap(): lax.ppermute(x, axis, [(i, i ^ bit) for i in range(lax.axis_size(axis))])  4.28 us
  transfers between devices with their start and end apart: 23, of which 16 were waited for; matrix products, arithmetic and copies ran while one was open for 0% of the time, Pallas kernels for 5%

profile of v2, /device:TPU:0, one launch (start us, length us, event | category | flops | bytes accessed | tf_op | source)
XLA Modules:
  0.0 77.0 jit_solution(6465888572090282396)
XLA Ops:
  2.2 3.5 %collective-permute-start.1 = (f32[2,8,128]{2,1,0:T(8,128)S(1)}, f32[2,8,128]{2,1,0:T(8,128)S(1)}, u32[]{:S(2)}, u32[]{:S(2)}) collective-permute-start(f32[2,8,128]{2,1,0:T(8,128)S(1)} %get-tuple-element.75.far), channel_id=1, source_target_pairs={{4,8},{8,4},{12,16},{16,12},{20,24},{24,20},{28,0},{0,28},{5,9},{9... | collective-permute-start | bytes 24584 | tf_op jit(solution)/shard_map/ppermute | solution.py:930
  5.7 1.4 %collective-permute-done.1.from_far = f32[2,8,128]{2,1,0:T(8,128)S(1)} collective-permute-done((f32[2,8,128]{2,1,0:T(8,128)S(1)}, f32[2,8,128]{2,1,0:T(8,128)S(1)}, u32[]{:S(2)}, u32[]{:S(2)}) %collective-permute-start.1) | collective-permute-done | bytes 8224 | tf_op jit(solution)/shard_map/ppermute | solution.py:930
  7.1 1.8 %collective-permute-start.2 = (f32[2,8,128]{2,1,0:T(8,128)S(1)}, f32[2,8,128]{2,1,0:T(8,128)S(1)}, u32[]{:S(2)}, u32[]{:S(2)}) collective-permute-start(f32[2,8,128]{2,1,0:T(8,128)S(1)} %get-tuple-element.76.near), channel_id=1, source_target_pairs={{0,1},{1,0},{2,3},{3,2},{4,5},{5,4},{6,7},{7,6},{8,9},{9,8},{10,11... | collective-permute-start | bytes 24584 | tf_op jit(solution)/shard_map/ppermute | solution.py:931
  8.8 2.5 %collective-permute-start.3 = (f32[2,8,128]{2,1,0:T(8,128)S(1)}, f32[2,8,128]{2,1,0:T(8,128)S(1)}, u32[]{:S(2)}, u32[]{:S(2)}) collective-permute-start(f32[2,8,128]{2,1,0:T(8,128)S(1)} %get-tuple-element.77.far), channel_id=1, source_target_pairs={{1,2},{2,1},{3,0},{0,3},{5,6},{6,5},{7,4},{4,7},{9,10},{10,9},{11,... | collective-permute-start | bytes 24584 | tf_op jit(solution)/shard_map/ppermute | solution.py:930
  12.0 1.9 %shard_map.277 = (f32[128,128]{1,0:T(8,128)S(1)}, bf16[1024,128]{1,0:T(8,128)(2,1)S(1)}, bf16[1024,128]{1,0:T(8,128)(2,1)S(1)}, bf16[896,256]{1,0:T(8,128)(2,1)S...) custom-call(f32[8,128]{1,0:T(8,128)} %table_h.1, ...), custom_call_target="tpu_custom_call" | custom-call | tf_op jit(solution)/shard_map/pallas_call | solution.py:31
  14.9 4.1 %shard_map.279 = (f32[2,8,128]{2,1,0:T(8,128)S(1)}, f32[2,8,128]{2,1,0:T(8,128)S(1)}, f32[4,8,128]{2,1,0:T(8,128)S(1)}, f32[8000,128]{1,0:T(8,128)S(1)}) custom-call(f32[2,8,128]{2,1,0:T(8,128)S(1)} %get-tuple-element.76.near, f32[2,8,128]{2,1,0:T(8,128)S(1)} %get-tuple-element.77.far, f32[2,8,128]{2,1,0:T(8,128)S(1)} %collective-permute-done.2.from_near, ...), custom_call_target="tpu_custom_call" | custom-call | tf_op jit(solution)/shard_map/pallas_call | solution.py:31
  19.1 2.0 %collective-permute-start.5 = (f32[2,8,128]{2,1,0:T(8,128)S(1)}, f32[2,8,128]{2,1,0:T(8,128)S(1)}, u32[]{:S(2)}, u32[]{:S(2)}) collective-permute-start(f32[2,8,128]{2,1,0:T(8,128)S(1)} %get-tuple-element.91.far), channel_id=1, source_target_pairs={{4,8},{8,4},{12,16},{16,12},{20,24},{24,20},{28,0},{0,28},{5,9},{9... | collective-permute-start | bytes 24584 | tf_op jit(solution)/shard_map/ppermute | solution.py:930
  21.0 2.1 %collective-permute-done.5.from_far = f32[2,8,128]{2,1,0:T(8,128)S(1)} collective-permute-done((f32[2,8,128]{2,1,0:T(8,128)S(1)}, f32[2,8,128]{2,1,0:T(8,128)S(1)}, u32[]{:S(2)}, u32[]{:S(2)}) %collective-permute-start.5) | collective-permute-done | bytes 8224 | tf_op jit(solution)/shard_map/ppermute | solution.py:930
  25.1 1.8 %collective-permute-done.6.from_near = f32[2,8,128]{2,1,0:T(8,128)S(1)} collective-permute-done((f32[2,8,128]{2,1,0:T(8,128)S(1)}, f32[2,8,128]{2,1,0:T(8,128)S(1)}, u32[]{:S(2)}, u32[]{:S(2)}) %collective-permute-start.6) | collective-permute-done | bytes 8224 | tf_op jit(solution)/shard_map/ppermute | solution.py:931
  26.8 2.5 %collective-permute-done.7.from_far = f32[2,8,128]{2,1,0:T(8,128)S(1)} collective-permute-done((f32[2,8,128]{2,1,0:T(8,128)S(1)}, f32[2,8,128]{2,1,0:T(8,128)S(1)}, u32[]{:S(2)}, u32[]{:S(2)}) %collective-permute-start.7) | collective-permute-done | bytes 8224 | tf_op jit(solution)/shard_map/ppermute | solution.py:930
  29.7 9.6 %all_to_all.5 = f32[32,1,128]{2,1,0:T(1,128)S(1)} all-to-all(f32[32,1,128]{2,1,0:T(1,128)S(1)} %bitcast.17), channel_id=1, replica_groups=mesh['slab'=8,'cross'=4] {'slab','cross'}, dimensions={0} | all-to-all | bytes 32768 | tf_op jit(solution)/shard_map/all_to_all | solution.py:1087
  40.9 2.9 %collective-permute-done.9.from_far = f32[2,8,128]{2,1,0:T(8,128)S(1)} collective-permute-done((f32[2,8,128]{2,1,0:T(8,128)S(1)}, f32[2,8,128]{2,1,0:T(8,128)S(1)}, u32[]{:S(2)}, u32[]{:S(2)}) %collective-permute-start.9) | collective-permute-done | bytes 8224 | tf_op jit(solution)/shard_map/ppermute | solution.py:930
  44.3 1.5 %collective-permute-start.11 = (f32[2,8,128]{2,1,0:T(8,128)S(1)}, f32[2,8,128]{2,1,0:T(8,128)S(1)}, u32[]{:S(2)}, u32[]{:S(2)}) collective-permute-start(f32[2,8,128]{2,1,0:T(8,128)S(1)} %get-tuple-element.101.far), channel_id=1, source_target_pairs={{1,2},{2,1},{3,0},{0,3},{5,6},{6,5},{7,4},{4,7},{9,10},{10,9},{11,... | collective-permute-start | bytes 24584 | tf_op jit(solution)/shard_map/ppermute | solution.py:930
  45.8 1.7 %collective-permute-done.10.from_near = f32[2,8,128]{2,1,0:T(8,128)S(1)} collective-permute-done((f32[2,8,128]{2,1,0:T(8,128)S(1)}, f32[2,8,128]{2,1,0:T(8,128)S(1)}, u32[]{:S(2)}, u32[]{:S(2)}) %collective-permute-start.10) | collective-permute-done | bytes 8224 | tf_op jit(solution)/shard_map/ppermute | solution.py:931
  47.5 2.3 %collective-permute-done.11.from_far = f32[2,8,128]{2,1,0:T(8,128)S(1)} collective-permute-done((f32[2,8,128]{2,1,0:T(8,128)S(1)}, f32[2,8,128]{2,1,0:T(8,128)S(1)}, u32[]{:S(2)}, u32[]{:S(2)}) %collective-permute-start.11) | collective-permute-done | bytes 8224 | tf_op jit(solution)/shard_map/ppermute | solution.py:930
  49.8 4.1 %shard_map.284 = (f32[4,128,128]{2,1,0:T(8,128)S(1)}, f32[4,128,128]{2,1,0:T(8,128)S(1)}, f32[4,8,128]{2,1,0:T(8,128)S(1)}, f32[576,128]{1,0:T(8,128)S(1)}) custom-call(f32[4,8,128]{2,1,0:T(8,128)S(1)} %get-tuple-element.89.pool, f32[2,8,128]{2,1,0:T(8,128)S(1)} %get-tuple-element.100.near, f32[2,8,128]{2,1,0:T(8,128)S(1)} %get-tuple-element.101.far, ...), custom_call_target="tpu_custom_call" | custom-call | tf_op jit(solution)/shard_map/pallas_call | solution.py:31
  56.8 3.0 %collective-permute-done.15.from_far = f32[2,8,128]{2,1,0:T(8,128)S(1)} collective-permute-done((f32[2,8,128]{2,1,0:T(8,128)S(1)}, f32[2,8,128]{2,1,0:T(8,128)S(1)}, u32[]{:S(2)}, u32[]{:S(2)}) %collective-permute-start.15) | collective-permute-done | bytes 8224 | tf_op jit(solution)/shard_map/ppermute | solution.py:930
  59.9 1.3 %collective-permute-done.13.other = f32[2,128,128]{2,1,0:T(8,128)S(1)} collective-permute-done((f32[2,128,128]{2,1,0:T(8,128)S(1)}, f32[2,128,128]{2,1,0:T(8,128)S(1)}, u32[]{:S(2)}, u32[]{:S(2)}) %collective-permute-start.13) | collective-permute-done | bytes 131104 | tf_op jit(solution)/shard_map/ppermute | solution.py:941
  61.7 1.6 %collective-permute-start.17 = (f32[2,8,128]{2,1,0:T(8,128)S(1)}, f32[2,8,128]{2,1,0:T(8,128)S(1)}, u32[]{:S(2)}, u32[]{:S(2)}) collective-permute-start(f32[2,8,128]{2,1,0:T(8,128)S(1)} %get-tuple-element.116.near), channel_id=1, source_target_pairs={{0,1},{1,0},{2,3},{3,2},{4,5},{5,4},{6,7},{7,6},{8,9},{9,8},{10,11... | collective-permute-start | bytes 24584 | tf_op jit(solution)/shard_map/ppermute | solution.py:931
  63.4 2.3 %collective-permute-start.18 = (f32[2,8,128]{2,1,0:T(8,128)S(1)}, f32[2,8,128]{2,1,0:T(8,128)S(1)}, u32[]{:S(2)}, u32[]{:S(2)}) collective-permute-start(f32[2,8,128]{2,1,0:T(8,128)S(1)} %get-tuple-element.117.far), channel_id=1, source_target_pairs={{1,2},{2,1},{3,0},{0,3},{5,6},{6,5},{7,4},{4,7},{9,10},{10,9},{11,... | collective-permute-start | bytes 24584 | tf_op jit(solution)/shard_map/ppermute | solution.py:930
  65.7 3.1 %collective-permute-done.18.from_far = f32[2,8,128]{2,1,0:T(8,128)S(1)} collective-permute-done((f32[2,8,128]{2,1,0:T(8,128)S(1)}, f32[2,8,128]{2,1,0:T(8,128)S(1)}, u32[]{:S(2)}, u32[]{:S(2)}) %collective-permute-start.18) | collective-permute-done | bytes 8224 | tf_op jit(solution)/shard_map/ppermute | solution.py:930
  70.0 2.3 %collective-permute-start.19 = (f32[128,128]{1,0:T(8,128)S(1)}, f32[128,128]{1,0:T(8,128)S(1)}, u32[]{:S(2)}, u32[]{:S(2)}) collective-permute-start(f32[128,128]{1,0:T(8,128)S(1)} %get-tuple-element.118.refs_0_), channel_id=1, source_target_pairs={{0,8},{4,12},{8,0},{12,4},{16,24},{20,28},{24,16},{28,20},{1,9},{5... | collective-permute-start | bytes 196616 | tf_op jit(solution)/shard_map/ppermute | solution.py:941
  72.4 1.7 %collective-permute-done.21.refs_3_ = f32[128,128]{1,0:T(8,128)S(1)} collective-permute-done((f32[128,128]{1,0:T(8,128)S(1)}, f32[128,128]{1,0:T(8,128)S(1)}, u32[]{:S(2)}, u32[]{:S(2)}) %collective-permute-start.21) | collective-permute-done | bytes 65568 | tf_op jit(solution)/shard_map/ppermute | solution.py:941
  74.7 1.2 %collective-permute-done.22.other = f32[128,128]{1,0:T(8,128)S(1)} collective-permute-done((f32[128,128]{1,0:T(8,128)S(1)}, f32[128,128]{1,0:T(8,128)S(1)}, u32[]{:S(2)}, u32[]{:S(2)}) %collective-permute-start.22) | collective-permute-done | bytes 65568 | tf_op jit(solution)/shard_map/ppermute | solution.py:941
  (39 shorter events, 13.5 us)
Async XLA Ops:
  1.6 4.1 %collective-permute-start = (f32[2,8,128]{2,1,0:T(8,128)S(1)}, f32[2,8,128]{2,1,0:T(8,128)S(1)}, u32[]{:S(2)}, u32[]{:S(2)}) collective-permute-start(f32[2,8,128]{2,1,0:T(8,128)S(1)} %get-tuple-element.74.near), channel_id=1, source_target_pairs={{0,4},{4,0},{8,12},{12,8},{16,20},{20,16},{24,28},{28,24},{1,5},{5... | collective-permute-start | bytes 24584 | tf_op jit(solution)/shard_map/ppermute | solution.py:931
  2.2 4.9 %collective-permute-start.1 = (f32[2,8,128]{2,1,0:T(8,128)S(1)}, f32[2,8,128]{2,1,0:T(8,128)S(1)}, u32[]{:S(2)}, u32[]{:S(2)}) collective-permute-start(f32[2,8,128]{2,1,0:T(8,128)S(1)} %get-tuple-element.75.far), channel_id=1, source_target_pairs={{4,8},{8,4},{12,16},{16,12},{20,24},{24,20},{28,0},{0,28},{5,9},{9... | collective-permute-start | bytes 24584 | tf_op jit(solution)/shard_map/ppermute | solution.py:930
  7.1 7.8 %collective-permute-start.2 = (f32[2,8,128]{2,1,0:T(8,128)S(1)}, f32[2,8,128]{2,1,0:T(8,128)S(1)}, u32[]{:S(2)}, u32[]{:S(2)}) collective-permute-start(f32[2,8,128]{2,1,0:T(8,128)S(1)} %get-tuple-element.76.near), channel_id=1, source_target_pairs={{0,1},{1,0},{2,3},{3,2},{4,5},{5,4},{6,7},{7,6},{8,9},{9,8},{10,11... | collective-permute-start | bytes 24584 | tf_op jit(solution)/shard_map/ppermute | solution.py:931
  8.8 6.1 %collective-permute-start.3 = (f32[2,8,128]{2,1,0:T(8,128)S(1)}, f32[2,8,128]{2,1,0:T(8,128)S(1)}, u32[]{:S(2)}, u32[]{:S(2)}) collective-permute-start(f32[2,8,128]{2,1,0:T(8,128)S(1)} %get-tuple-element.77.far), channel_id=1, source_target_pairs={{1,2},{2,1},{3,0},{0,3},{5,6},{6,5},{7,4},{4,7},{9,10},{10,9},{11,... | collective-permute-start | bytes 24584 | tf_op jit(solution)/shard_map/ppermute | solution.py:930
  19.0 2.0 %collective-permute-start.4 = (f32[2,8,128]{2,1,0:T(8,128)S(1)}, f32[2,8,128]{2,1,0:T(8,128)S(1)}, u32[]{:S(2)}, u32[]{:S(2)}) collective-permute-start(f32[2,8,128]{2,1,0:T(8,128)S(1)} %get-tuple-element.90.near), channel_id=1, source_target_pairs={{0,4},{4,0},{8,12},{12,8},{16,20},{20,16},{24,28},{28,24},{1,5},{5... | collective-permute-start | bytes 24584 | tf_op jit(solution)/shard_map/ppermute | solution.py:931
  19.1 4.0 %collective-permute-start.5 = (f32[2,8,128]{2,1,0:T(8,128)S(1)}, f32[2,8,128]{2,1,0:T(8,128)S(1)}, u32[]{:S(2)}, u32[]{:S(2)}) collective-permute-start(f32[2,8,128]{2,1,0:T(8,128)S(1)} %get-tuple-element.91.far), channel_id=1, source_target_pairs={{4,8},{8,4},{12,16},{16,12},{20,24},{24,20},{28,0},{0,28},{5,9},{9... | collective-permute-start | bytes 24584 | tf_op jit(solution)/shard_map/ppermute | solution.py:930
  23.1 3.7 %collective-permute-start.6 = (f32[2,8,128]{2,1,0:T(8,128)S(1)}, f32[2,8,128]{2,1,0:T(8,128)S(1)}, u32[]{:S(2)}, u32[]{:S(2)}) collective-permute-start(f32[2,8,128]{2,1,0:T(8,128)S(1)} %get-tuple-element.92.near), channel_id=1, source_target_pairs={{0,1},{1,0},{2,3},{3,2},{4,5},{5,4},{6,7},{7,6},{8,9},{9,8},{10,11... | collective-permute-start | bytes 24584 | tf_op jit(solution)/shard_map/ppermute | solution.py:931
  23.8 5.4 %collective-permute-start.7 = (f32[2,8,128]{2,1,0:T(8,128)S(1)}, f32[2,8,128]{2,1,0:T(8,128)S(1)}, u32[]{:S(2)}, u32[]{:S(2)}) collective-permute-start(f32[2,8,128]{2,1,0:T(8,128)S(1)} %get-tuple-element.93.far), channel_id=1, source_target_pairs={{1,2},{2,1},{3,0},{0,3},{5,6},{6,5},{7,4},{4,7},{9,10},{10,9},{11,... | collective-permute-start | bytes 24584 | tf_op jit(solution)/shard_map/ppermute | solution.py:930
  39.6 1.2 %collective-permute-start.8 = (f32[2,8,128]{2,1,0:T(8,128)S(1)}, f32[2,8,128]{2,1,0:T(8,128)S(1)}, u32[]{:S(2)}, u32[]{:S(2)}) collective-permute-start(f32[2,8,128]{2,1,0:T(8,128)S(1)} %get-tuple-element.98.near), channel_id=1, source_target_pairs={{0,4},{4,0},{8,12},{12,8},{16,20},{20,16},{24,28},{28,24},{1,5},{5... | collective-permute-start | bytes 24584 | tf_op jit(solution)/shard_map/ppermute | solution.py:931
  39.7 4.0 %collective-permute-start.9 = (f32[2,8,128]{2,1,0:T(8,128)S(1)}, f32[2,8,128]{2,1,0:T(8,128)S(1)}, u32[]{:S(2)}, u32[]{:S(2)}) collective-permute-start(f32[2,8,128]{2,1,0:T(8,128)S(1)} %get-tuple-element.99.far), channel_id=1, source_target_pairs={{4,8},{8,4},{12,16},{16,12},{20,24},{24,20},{28,0},{0,28},{5,9},{9... | collective-permute-start | bytes 24584 | tf_op jit(solution)/shard_map/ppermute | solution.py:930
  43.8 3.7 %collective-permute-start.10 = (f32[2,8,128]{2,1,0:T(8,128)S(1)}, f32[2,8,128]{2,1,0:T(8,128)S(1)}, u32[]{:S(2)}, u32[]{:S(2)}) collective-permute-start(f32[2,8,128]{2,1,0:T(8,128)S(1)} %get-tuple-element.100.near), channel_id=1, source_target_pairs={{0,1},{1,0},{2,3},{3,2},{4,5},{5,4},{6,7},{7,6},{8,9},{9,8},{10,11... | collective-permute-start | bytes 24584 | tf_op jit(solution)/shard_map/ppermute | solution.py:931
  44.3 5.4 %collective-permute-start.11 = (f32[2,8,128]{2,1,0:T(8,128)S(1)}, f32[2,8,128]{2,1,0:T(8,128)S(1)}, u32[]{:S(2)}, u32[]{:S(2)}) collective-permute-start(f32[2,8,128]{2,1,0:T(8,128)S(1)} %get-tuple-element.101.far), channel_id=1, source_target_pairs={{1,2},{2,1},{3,0},{0,3},{5,6},{6,5},{7,4},{4,7},{9,10},{10,9},{11,... | collective-permute-start | bytes 24584 | tf_op jit(solution)/shard_map/ppermute | solution.py:930
  53.9 1.6 %collective-permute-start.12 = (f32[4,128,128]{2,1,0:T(8,128)S(1)}, f32[4,128,128]{2,1,0:T(8,128)S(1)}, u32[]{:S(2)}, u32[]{:S(2)}) collective-permute-start(f32[4,128,128]{2,1,0:T(8,128)S(1)} %get-tuple-element.106), channel_id=1, source_target_pairs={{0,4},{4,0},{8,12},{12,8},{16,20},{20,16},{24,28},{28,24},{1,5},{5... | collective-permute-start | bytes 786440 | tf_op jit(solution)/shard_map/ppermute | solution.py:941
  55.5 5.7 %collective-permute-start.13 = (f32[2,128,128]{2,1,0:T(8,128)S(1)}, f32[2,128,128]{2,1,0:T(8,128)S(1)}, u32[]{:S(2)}, u32[]{:S(2)}) collective-permute-start(f32[2,128,128]{2,1,0:T(8,128)S(1)} %get-tuple-element.111), channel_id=1, source_target_pairs={{0,1},{1,0},{2,3},{3,2},{4,5},{5,4},{6,7},{7,6},{8,9},{9,8},{10,11... | collective-permute-start | bytes 393224 | tf_op jit(solution)/shard_map/ppermute | solution.py:941
  55.6 1.2 %collective-permute-start.14 = (f32[2,8,128]{2,1,0:T(8,128)S(1)}, f32[2,8,128]{2,1,0:T(8,128)S(1)}, u32[]{:S(2)}, u32[]{:S(2)}) collective-permute-start(f32[2,8,128]{2,1,0:T(8,128)S(1)} %get-tuple-element.112.near), channel_id=1, source_target_pairs={{0,4},{4,0},{8,12},{12,8},{16,20},{20,16},{24,28},{28,24},{1,5},{5... | collective-permute-start | bytes 24584 | tf_op jit(solution)/shard_map/ppermute | solution.py:931
  55.9 4.0 %collective-permute-start.15 = (f32[2,8,128]{2,1,0:T(8,128)S(1)}, f32[2,8,128]{2,1,0:T(8,128)S(1)}, u32[]{:S(2)}, u32[]{:S(2)}) collective-permute-start(f32[2,8,128]{2,1,0:T(8,128)S(1)} %get-tuple-element.113.far), channel_id=1, source_target_pairs={{4,8},{8,4},{12,16},{16,12},{20,24},{24,20},{28,0},{0,28},{5,9},{9... | collective-permute-start | bytes 24584 | tf_op jit(solution)/shard_map/ppermute | solution.py:930
  61.2 7.6 %collective-permute-start.16 = (f32[1,128,128]{2,1,0:T(8,128)S(1)}, f32[1,128,128]{2,1,0:T(8,128)S(1)}, u32[]{:S(2)}, u32[]{:S(2)}) collective-permute-start(f32[1,128,128]{2,1,0:T(8,128)S(1)} %get-tuple-element.115), channel_id=1, source_target_pairs={{0,2},{1,3},{2,0},{3,1},{4,6},{5,7},{6,4},{7,5},{8,10},{9,11},{10,... | collective-permute-start | bytes 196616 | tf_op jit(solution)/shard_map/ppermute | solution.py:941
  61.7 3.9 %collective-permute-start.17 = (f32[2,8,128]{2,1,0:T(8,128)S(1)}, f32[2,8,128]{2,1,0:T(8,128)S(1)}, u32[]{:S(2)}, u32[]{:S(2)}) collective-permute-start(f32[2,8,128]{2,1,0:T(8,128)S(1)} %get-tuple-element.116.near), channel_id=1, source_target_pairs={{0,1},{1,0},{2,3},{3,2},{4,5},{5,4},{6,7},{7,6},{8,9},{9,8},{10,11... | collective-permute-start | bytes 24584 | tf_op jit(solution)/shard_map/ppermute | solution.py:931
  63.4 5.4 %collective-permute-start.18 = (f32[2,8,128]{2,1,0:T(8,128)S(1)}, f32[2,8,128]{2,1,0:T(8,128)S(1)}, u32[]{:S(2)}, u32[]{:S(2)}) collective-permute-start(f32[2,8,128]{2,1,0:T(8,128)S(1)} %get-tuple-element.117.far), channel_id=1, source_target_pairs={{1,2},{2,1},{3,0},{0,3},{5,6},{6,5},{7,4},{4,7},{9,10},{10,9},{11,... | collective-permute-start | bytes 24584 | tf_op jit(solution)/shard_map/ppermute | solution.py:930
  68.8 5.2 %collective-permute-start.21 = (f32[128,128]{1,0:T(8,128)S(1)}, f32[128,128]{1,0:T(8,128)S(1)}, u32[]{:S(2)}, u32[]{:S(2)}) collective-permute-start(f32[128,128]{1,0:T(8,128)S(1)} %get-tuple-element.118.refs_0_), channel_id=1, source_target_pairs={{0,24},{4,28},{8,16},{12,20},{16,8},{20,12},{24,0},{28,4},{1,25},{... | collective-permute-start | bytes 196616 | tf_op jit(solution)/shard_map/ppermute | solution.py:941
  68.9 5.2 %collective-permute-start.20 = (f32[128,128]{1,0:T(8,128)S(1)}, f32[128,128]{1,0:T(8,128)S(1)}, u32[]{:S(2)}, u32[]{:S(2)}) collective-permute-start(f32[128,128]{1,0:T(8,128)S(1)} %get-tuple-element.118.refs_0_), channel_id=1, source_target_pairs={{0,16},{4,20},{8,24},{12,28},{16,0},{20,4},{24,8},{28,12},{1,17},{... | collective-permute-start | bytes 196616 | tf_op jit(solution)/shard_map/ppermute | solution.py:941
  70.0 4.6 %collective-permute-start.19 = (f32[128,128]{1,0:T(8,128)S(1)}, f32[128,128]{1,0:T(8,128)S(1)}, u32[]{:S(2)}, u32[]{:S(2)}) collective-permute-start(f32[128,128]{1,0:T(8,128)S(1)} %get-tuple-element.118.refs_0_), channel_id=1, source_target_pairs={{0,8},{4,12},{8,0},{12,4},{16,24},{20,28},{24,16},{28,20},{1,9},{5... | collective-permute-start | bytes 196616 | tf_op jit(solution)/shard_map/ppermute | solution.py:941
  74.7 1.3 %collective-permute-start.22 = (f32[128,128]{1,0:T(8,128)S(1)}, f32[128,128]{1,0:T(8,128)S(1)}, u32[]{:S(2)}, u32[]{:S(2)}) collective-permute-start(f32[128,128]{1,0:T(8,128)S(1)} %shard_map.289.mine), channel_id=1, source_target_pairs={{0,4},{4,0},{8,12},{12,8},{16,20},{20,16},{24,28},{28,24},{1,5},{5... | collective-permute-start | bytes 196616 | tf_op jit(solution)/shard_map/ppermute | solution.py:941

commit v3 on v2

--- a/solution.py
+++ b/solution.py
@@ -941,34 +941,8 @@
     return lax.ppermute(x, axis, [(i, i ^ bit) for i in range(lax.axis_size(axis))])
 
 
-def halve(bit, x, other, keep, send):
-    mine = (lax.axis_index("cross") // bit) % 2
-    shape = (x.shape[0] // 2, 2) + x.shape[1:]
-    x, other = x.reshape(shape), other.reshape(shape)
-    for ref, side in ((keep, mine), (send, 1 - mine)):
-        value = x[:, pl.ds(side, 1)] + other[:, pl.ds(side, 1)]
-        ref[...] = value.reshape(ref.shape)
-
-
-def halve_hold_body(bit, x, other, near, far, keep, send, near_out, far_out):
-    halve(bit, x, other, keep, send)
-    near_out[...] = near[...]
-    far_out[...] = far[...]
-
-
-def halve_turn_body(bit, x, other, near, far, from_near, from_far, keep, send, near_out, far_out):
-    halve(bit, x, other, keep, send)
-    turn_body(near, far, from_near, from_far, near_out, far_out)
-
-
 def add_body(x, other, out):
     out[...] = x[...] + other[...]
-
-
-def add_sides_body(x, other, near, far, from_near, from_far, out, near_out, far_out):
-    add_body(x, other, out)
-    add_body(near, from_near, near_out)
-    add_body(far, from_far, far_out)
 
 
 def add_all_body(*refs):
@@ -978,35 +952,46 @@
     refs[-1][...] = total
 
 
+def spread_body(x, other, near, far, *outs):
+    me = lax.axis_index("cross")
+    for step, ref in enumerate(outs[:-2]):
+        part = pl.ds(me ^ step, 1)
+        ref[...] = (x[part] + other[part]).reshape(ref.shape)
+    outs[-2][...] = near[...]
+    outs[-1][...] = far[...]
+
+
+def gather_turn_body(near, far, from_near, from_far, *refs):
+    add_all_body(*refs[:-2])
+    turn_body(near, far, from_near, from_far, refs[-2], refs[-1])
+
+
+def gather_sides_body(near, far, from_near, from_far, *refs):
+    add_all_body(*refs[:-2])
+    add_body(near, from_near, refs[-2])
+    add_body(far, from_far, refs[-1])
+
+
 def reduce_all(keep, send, near, far):
     slab_count, cross_count = lax.axis_size("slab"), lax.axis_size("cross")
-    group = (near.shape, f32)
-    other = swap(send, "slab", 1)
-    bit, step, received = 1, 0, None
-    while bit < cross_count:
-        half = ((keep.shape[0] // 2,) + keep.shape[1:], f32)
-        if step == 0:
-            keep, send, near, far = call(
-                functools.partial(halve_hold_body, bit), [half, half, group, group], keep, other, near, far
-            )
-            received = neighbours_swap(near, far, "slab")
-        elif step == 1:
-            keep, send, near, far = call(
-                functools.partial(halve_turn_body, bit), [half, half, group, group],
-                keep, other, near, far, *received,
-            )
-            received = neighbours_swap(near, far, "cross")
-        else:
-            raise NotImplementedError
-        other = swap(send, "cross", bit)
-        bit, step = 2 * bit, step + 1
-    x, other = keep[0], other[0]
-    x, *sides = call(add_sides_body, [(x.shape, f32), group, group], x, other, near, far, *received)
+    group, part = (near.shape, f32), (keep.shape[1:], f32)
+    *shares, near, far = call(
+        spread_body, [part] * cross_count + [group] * 2, keep, swap(send, "slab", 1), near, far
+    )
+    got = [swap(shares[step], "cross", step) for step in range(1, cross_count)]
+    received = neighbours_swap(near, far, "slab")
+    x, near, far = call(gather_turn_body, [part, group, group], near, far, *received, shares[0], *got)
+    received = neighbours_swap(near, far, "cross")
     bits = [2**b for b in range(1, slab_count.bit_length()) if 2**b < slab_count]
+    sides = None
     for i in range(0, len(bits), 2):
         pair = bits[i : i + 2]
         steps = pair + [sum(pair)] * (len(pair) - 1)
-        (x,) = call(add_all_body, [(x.shape, f32)], x, *[swap(x, "slab", step) for step in steps])
+        parts = [x] + [swap(x, "slab", step) for step in steps]
+        if sides is None:
+            x, *sides = call(gather_sides_body, [part, group, group], near, far, *received, *parts)
+        else:
+            (x,) = call(add_all_body, [part], *parts)
     return x, swap(x, "slab", 1), sides
 
 

time: 77.4 us -> 77.3 us (level)
  waiting for transfers between devices: 27.3 us -> 24.7 us
  starting transfers between devices: 23.6 us -> 26.1 us
    ppermute x7 -> x8, starting transfers between devices: 4.28 us -> 8.13 us  [swap(): lax.ppermute(x, axis, [(i, i ^ bit) for i in range(lax.axis_size(axis))])]
    ppermute x7 -> x8, waiting for transfers between devices: 5.16 us -> 1.89 us  [swap(): lax.ppermute(x, axis, [(i, i ^ bit) for i in range(lax.axis_size(axis))])]
    ppermute x8, waiting for transfers between devices: 4.89 us -> 5.9 us  [neighbours_swap(): from_near = lax.ppermute(near, axis, pairs[0])]
    pallas_call x16 -> x15, Pallas kernels: 15.2 us -> 15.2 us  [call(): pl.pallas_call(body, out_shape=[(pltpu.VMEM if keep else jax.ShapeDtypeSt...]
  transfers between devices with their start and end apart: 23 -> 24, of which waited for: 16 -> 15; matrix products, arithmetic and copies ran while one was open for 0% -> 0% of each run, Pallas kernels for 5% -> 5%
where the time goes in v3:
time: 77.3 us; the launch traced here: 77 us
  starting transfers between devices  26.1 us (34%)
  waiting for transfers between devices  24.7 us (32%)
  Pallas kernels  15.2 us (20%)
  blocking collectives  9.55 us (12%)
  between operations  1.44 us (2%)
    ppermute x8, waiting for transfers between devices, neighbours_swap(): from_far = lax.ppermute(far, axis, pairs[1])  16.9 us
    pallas_call x15, Pallas kernels, call(): pl.pallas_call(body, out_shape=[(pltpu.VMEM if keep else jax.ShapeDtypeSt...  15.2 us
    ppermute x8, starting transfers between devices, neighbours_swap(): from_far = lax.ppermute(far, axis, pairs[1])  13 us
    all_to_all x1, blocking collectives, device_step(): lax.all_to_all(hist.reshape(devices, 1, bin_total), ('slab', 'cross'), 0, 0)  9.55 us
    ppermute x8, starting transfers between devices, swap(): lax.ppermute(x, axis, [(i, i ^ bit) for i in range(lax.axis_size(axis))])  8.13 us
    ppermute x8, waiting for transfers between devices, neighbours_swap(): from_near = lax.ppermute(near, axis, pairs[0])  5.9 us
    ppermute x8, starting transfers between devices, neighbours_swap(): from_near = lax.ppermute(near, axis, pairs[0])  4.96 us
    ppermute x8, waiting for transfers between devices, swap(): lax.ppermute(x, axis, [(i, i ^ bit) for i in range(lax.axis_size(axis))])  1.89 us
  transfers between devices with their start and end apart: 24, of which 15 were waited for; matrix products, arithmetic and copies ran while one was open for 0% of the time, Pallas kernels for 5%

profile of v3, /device:TPU:0, one launch (start us, length us, event | category | flops | bytes accessed | tf_op | source)
XLA Modules:
  0.0 77.0 jit_solution(16559994667511481395)
XLA Ops:
  2.2 3.5 %collective-permute-start.1 = (f32[2,8,128]{2,1,0:T(8,128)S(1)}, f32[2,8,128]{2,1,0:T(8,128)S(1)}, u32[]{:S(2)}, u32[]{:S(2)}) collective-permute-start(f32[2,8,128]{2,1,0:T(8,128)S(1)} %get-tuple-element.76.far), channel_id=1, source_target_pairs={{4,8},{8,4},{12,16},{16,12},{20,24},{24,20},{28,0},{0,28},{5,9},{9... | collective-permute-start | bytes 24584 | tf_op jit(solution)/shard_map/ppermute | solution.py:930
  5.7 1.4 %collective-permute-done.1.from_far = f32[2,8,128]{2,1,0:T(8,128)S(1)} collective-permute-done((f32[2,8,128]{2,1,0:T(8,128)S(1)}, f32[2,8,128]{2,1,0:T(8,128)S(1)}, u32[]{:S(2)}, u32[]{:S(2)}) %collective-permute-start.1) | collective-permute-done | bytes 8224 | tf_op jit(solution)/shard_map/ppermute | solution.py:930
  7.1 1.8 %collective-permute-start.2 = (f32[2,8,128]{2,1,0:T(8,128)S(1)}, f32[2,8,128]{2,1,0:T(8,128)S(1)}, u32[]{:S(2)}, u32[]{:S(2)}) collective-permute-start(f32[2,8,128]{2,1,0:T(8,128)S(1)} %get-tuple-element.77.near), channel_id=1, source_target_pairs={{0,1},{1,0},{2,3},{3,2},{4,5},{5,4},{6,7},{7,6},{8,9},{9,8},{10,11... | collective-permute-start | bytes 24584 | tf_op jit(solution)/shard_map/ppermute | solution.py:931
  8.8 2.5 %collective-permute-start.3 = (f32[2,8,128]{2,1,0:T(8,128)S(1)}, f32[2,8,128]{2,1,0:T(8,128)S(1)}, u32[]{:S(2)}, u32[]{:S(2)}) collective-permute-start(f32[2,8,128]{2,1,0:T(8,128)S(1)} %get-tuple-element.78.far), channel_id=1, source_target_pairs={{1,2},{2,1},{3,0},{0,3},{5,6},{6,5},{7,4},{4,7},{9,10},{10,9},{11,... | collective-permute-start | bytes 24584 | tf_op jit(solution)/shard_map/ppermute | solution.py:930
  12.0 1.9 %shard_map.277 = (f32[128,128]{1,0:T(8,128)S(1)}, bf16[1024,128]{1,0:T(8,128)(2,1)S(1)}, bf16[1024,128]{1,0:T(8,128)(2,1)S(1)}, bf16[896,256]{1,0:T(8,128)(2,1)S...) custom-call(f32[8,128]{1,0:T(8,128)} %table_h.1, ...), custom_call_target="tpu_custom_call" | custom-call | tf_op jit(solution)/shard_map/pallas_call | solution.py:31
  14.9 4.1 %shard_map.279 = (f32[2,8,128]{2,1,0:T(8,128)S(1)}, f32[2,8,128]{2,1,0:T(8,128)S(1)}, f32[4,8,128]{2,1,0:T(8,128)S(1)}, f32[8000,128]{1,0:T(8,128)S(1)}) custom-call(f32[2,8,128]{2,1,0:T(8,128)S(1)} %get-tuple-element.77.near, f32[2,8,128]{2,1,0:T(8,128)S(1)} %get-tuple-element.78.far, f32[2,8,128]{2,1,0:T(8,128)S(1)} %collective-permute-done.2.from_near, ...), custom_call_target="tpu_custom_call" | custom-call | tf_op jit(solution)/shard_map/pallas_call | solution.py:31
  19.1 2.0 %collective-permute-start.5 = (f32[2,8,128]{2,1,0:T(8,128)S(1)}, f32[2,8,128]{2,1,0:T(8,128)S(1)}, u32[]{:S(2)}, u32[]{:S(2)}) collective-permute-start(f32[2,8,128]{2,1,0:T(8,128)S(1)} %get-tuple-element.92.far), channel_id=1, source_target_pairs={{4,8},{8,4},{12,16},{16,12},{20,24},{24,20},{28,0},{0,28},{5,9},{9... | collective-permute-start | bytes 24584 | tf_op jit(solution)/shard_map/ppermute | solution.py:930
  21.0 2.1 %collective-permute-done.5.from_far = f32[2,8,128]{2,1,0:T(8,128)S(1)} collective-permute-done((f32[2,8,128]{2,1,0:T(8,128)S(1)}, f32[2,8,128]{2,1,0:T(8,128)S(1)}, u32[]{:S(2)}, u32[]{:S(2)}) %collective-permute-start.5) | collective-permute-done | bytes 8224 | tf_op jit(solution)/shard_map/ppermute | solution.py:930
  25.1 1.8 %collective-permute-done.6.from_near = f32[2,8,128]{2,1,0:T(8,128)S(1)} collective-permute-done((f32[2,8,128]{2,1,0:T(8,128)S(1)}, f32[2,8,128]{2,1,0:T(8,128)S(1)}, u32[]{:S(2)}, u32[]{:S(2)}) %collective-permute-start.6) | collective-permute-done | bytes 8224 | tf_op jit(solution)/shard_map/ppermute | solution.py:931
  26.8 2.5 %collective-permute-done.7.from_far = f32[2,8,128]{2,1,0:T(8,128)S(1)} collective-permute-done((f32[2,8,128]{2,1,0:T(8,128)S(1)}, f32[2,8,128]{2,1,0:T(8,128)S(1)}, u32[]{:S(2)}, u32[]{:S(2)}) %collective-permute-start.7) | collective-permute-done | bytes 8224 | tf_op jit(solution)/shard_map/ppermute | solution.py:930
  29.7 9.6 %all_to_all.5 = f32[32,1,128]{2,1,0:T(1,128)S(1)} all-to-all(f32[32,1,128]{2,1,0:T(1,128)S(1)} %bitcast.13), channel_id=1, replica_groups=mesh['slab'=8,'cross'=4] {'slab','cross'}, dimensions={0} | all-to-all | bytes 32768 | tf_op jit(solution)/shard_map/all_to_all | solution.py:1072
  40.9 2.9 %collective-permute-done.9.from_far = f32[2,8,128]{2,1,0:T(8,128)S(1)} collective-permute-done((f32[2,8,128]{2,1,0:T(8,128)S(1)}, f32[2,8,128]{2,1,0:T(8,128)S(1)}, u32[]{:S(2)}, u32[]{:S(2)}) %collective-permute-start.9) | collective-permute-done | bytes 8224 | tf_op jit(solution)/shard_map/ppermute | solution.py:930
  44.3 1.5 %collective-permute-start.11 = (f32[2,8,128]{2,1,0:T(8,128)S(1)}, f32[2,8,128]{2,1,0:T(8,128)S(1)}, u32[]{:S(2)}, u32[]{:S(2)}) collective-permute-start(f32[2,8,128]{2,1,0:T(8,128)S(1)} %get-tuple-element.102.far), channel_id=1, source_target_pairs={{1,2},{2,1},{3,0},{0,3},{5,6},{6,5},{7,4},{4,7},{9,10},{10,9},{11,... | collective-permute-start | bytes 24584 | tf_op jit(solution)/shard_map/ppermute | solution.py:930
  45.8 1.7 %collective-permute-done.10.from_near = f32[2,8,128]{2,1,0:T(8,128)S(1)} collective-permute-done((f32[2,8,128]{2,1,0:T(8,128)S(1)}, f32[2,8,128]{2,1,0:T(8,128)S(1)}, u32[]{:S(2)}, u32[]{:S(2)}) %collective-permute-start.10) | collective-permute-done | bytes 8224 | tf_op jit(solution)/shard_map/ppermute | solution.py:931
  47.5 2.3 %collective-permute-done.11.from_far = f32[2,8,128]{2,1,0:T(8,128)S(1)} collective-permute-done((f32[2,8,128]{2,1,0:T(8,128)S(1)}, f32[2,8,128]{2,1,0:T(8,128)S(1)}, u32[]{:S(2)}, u32[]{:S(2)}) %collective-permute-start.11) | collective-permute-done | bytes 8224 | tf_op jit(solution)/shard_map/ppermute | solution.py:930
  49.8 4.1 %shard_map.284 = (f32[4,128,128]{2,1,0:T(8,128)S(1)}, f32[4,128,128]{2,1,0:T(8,128)S(1)}, f32[4,8,128]{2,1,0:T(8,128)S(1)}, f32[576,128]{1,0:T(8,128)S(1)}) custom-call(f32[4,8,128]{2,1,0:T(8,128)S(1)} %get-tuple-element.90.pool, f32[2,8,128]{2,1,0:T(8,128)S(1)} %get-tuple-element.101.near, f32[2,8,128]{2,1,0:T(8,128)S(1)} %get-tuple-element.102.far, ...), custom_call_target="tpu_custom_call" | custom-call | tf_op jit(solution)/shard_map/pallas_call | solution.py:31
  55.6 2.1 %collective-permute-start.16 = (f32[128,128]{1,0:T(8,128)S(1)}, f32[128,128]{1,0:T(8,128)S(1)}, u32[]{:S(2)}, u32[]{:S(2)}) collective-permute-start(f32[128,128]{1,0:T(8,128)S(1)} %get-tuple-element.115), channel_id=1, source_target_pairs={{0,2},{1,3},{2,0},{3,1},{4,6},{5,7},{6,4},{7,5},{8,10},{9,11},{10,... | collective-permute-start | bytes 196616 | tf_op jit(solution)/shard_map/ppermute | solution.py:941
  57.7 2.3 %collective-permute-start.17 = (f32[128,128]{1,0:T(8,128)S(1)}, f32[128,128]{1,0:T(8,128)S(1)}, u32[]{:S(2)}, u32[]{:S(2)}) collective-permute-start(f32[128,128]{1,0:T(8,128)S(1)} %get-tuple-element.116), channel_id=1, source_target_pairs={{0,3},{1,2},{2,1},{3,0},{4,7},{5,6},{6,5},{7,4},{8,11},{9,10},{10,... | collective-permute-start | bytes 196616 | tf_op jit(solution)/shard_map/ppermute | solution.py:941
  61.2 2.8 %collective-permute-done.14.from_far = f32[2,8,128]{2,1,0:T(8,128)S(1)} collective-permute-done((f32[2,8,128]{2,1,0:T(8,128)S(1)}, f32[2,8,128]{2,1,0:T(8,128)S(1)}, u32[]{:S(2)}, u32[]{:S(2)}) %collective-permute-start.14) | collective-permute-done | bytes 8224 | tf_op jit(solution)/shard_map/ppermute | solution.py:930
  65.5 2.3 %collective-permute-start.20 = (f32[128,128]{1,0:T(8,128)S(1)}, f32[128,128]{1,0:T(8,128)S(1)}, u32[]{:S(2)}, u32[]{:S(2)}) collective-permute-start(f32[128,128]{1,0:T(8,128)S(1)} %get-tuple-element.119.refs_0_), channel_id=1, source_target_pairs={{0,8},{4,12},{8,0},{12,4},{16,24},{20,28},{24,16},{28,20},{1,9},{5... | collective-permute-start | bytes 196616 | tf_op jit(solution)/shard_map/ppermute | solution.py:941
  67.9 1.3 %collective-permute-start.18 = (f32[2,8,128]{2,1,0:T(8,128)S(1)}, f32[2,8,128]{2,1,0:T(8,128)S(1)}, u32[]{:S(2)}, u32[]{:S(2)}) collective-permute-start(f32[2,8,128]{2,1,0:T(8,128)S(1)} %get-tuple-element.117.near), channel_id=1, source_target_pairs={{0,1},{1,0},{2,3},{3,2},{4,5},{5,4},{6,7},{7,6},{8,9},{9,8},{10,11... | collective-permute-start | bytes 24584 | tf_op jit(solution)/shard_map/ppermute | solution.py:931
  69.1 1.6 %collective-permute-start.19 = (f32[2,8,128]{2,1,0:T(8,128)S(1)}, f32[2,8,128]{2,1,0:T(8,128)S(1)}, u32[]{:S(2)}, u32[]{:S(2)}) collective-permute-start(f32[2,8,128]{2,1,0:T(8,128)S(1)} %get-tuple-element.118.far), channel_id=1, source_target_pairs={{1,2},{2,1},{3,0},{0,3},{5,6},{6,5},{7,4},{4,7},{9,10},{10,9},{11,... | collective-permute-start | bytes 24584 | tf_op jit(solution)/shard_map/ppermute | solution.py:930
  71.5 3.0 %collective-permute-done.19.from_far = f32[2,8,128]{2,1,0:T(8,128)S(1)} collective-permute-done((f32[2,8,128]{2,1,0:T(8,128)S(1)}, f32[2,8,128]{2,1,0:T(8,128)S(1)}, u32[]{:S(2)}, u32[]{:S(2)}) %collective-permute-start.19) | collective-permute-done | bytes 8224 | tf_op jit(solution)/shard_map/ppermute | solution.py:930
  74.7 1.2 %collective-permute-done.23.other = f32[128,128]{1,0:T(8,128)S(1)} collective-permute-done((f32[128,128]{1,0:T(8,128)S(1)}, f32[128,128]{1,0:T(8,128)S(1)}, u32[]{:S(2)}, u32[]{:S(2)}) %collective-permute-start.23) | collective-permute-done | bytes 65568 | tf_op jit(solution)/shard_map/ppermute | solution.py:941
  (40 shorter events, 13.4 us)
Async XLA Ops:
  1.6 4.1 %collective-permute-start = (f32[2,8,128]{2,1,0:T(8,128)S(1)}, f32[2,8,128]{2,1,0:T(8,128)S(1)}, u32[]{:S(2)}, u32[]{:S(2)}) collective-permute-start(f32[2,8,128]{2,1,0:T(8,128)S(1)} %get-tuple-element.75.near), channel_id=1, source_target_pairs={{0,4},{4,0},{8,12},{12,8},{16,20},{20,16},{24,28},{28,24},{1,5},{5... | collective-permute-start | bytes 24584 | tf_op jit(solution)/shard_map/ppermute | solution.py:931
  2.2 4.9 %collective-permute-start.1 = (f32[2,8,128]{2,1,0:T(8,128)S(1)}, f32[2,8,128]{2,1,0:T(8,128)S(1)}, u32[]{:S(2)}, u32[]{:S(2)}) collective-permute-start(f32[2,8,128]{2,1,0:T(8,128)S(1)} %get-tuple-element.76.far), channel_id=1, source_target_pairs={{4,8},{8,4},{12,16},{16,12},{20,24},{24,20},{28,0},{0,28},{5,9},{9... | collective-permute-start | bytes 24584 | tf_op jit(solution)/shard_map/ppermute | solution.py:930
  7.1 7.8 %collective-permute-start.2 = (f32[2,8,128]{2,1,0:T(8,128)S(1)}, f32[2,8,128]{2,1,0:T(8,128)S(1)}, u32[]{:S(2)}, u32[]{:S(2)}) collective-permute-start(f32[2,8,128]{2,1,0:T(8,128)S(1)} %get-tuple-element.77.near), channel_id=1, source_target_pairs={{0,1},{1,0},{2,3},{3,2},{4,5},{5,4},{6,7},{7,6},{8,9},{9,8},{10,11... | collective-permute-start | bytes 24584 | tf_op jit(solution)/shard_map/ppermute | solution.py:931
  8.8 6.1 %collective-permute-start.3 = (f32[2,8,128]{2,1,0:T(8,128)S(1)}, f32[2,8,128]{2,1,0:T(8,128)S(1)}, u32[]{:S(2)}, u32[]{:S(2)}) collective-permute-start(f32[2,8,128]{2,1,0:T(8,128)S(1)} %get-tuple-element.78.far), channel_id=1, source_target_pairs={{1,2},{2,1},{3,0},{0,3},{5,6},{6,5},{7,4},{4,7},{9,10},{10,9},{11,... | collective-permute-start | bytes 24584 | tf_op jit(solution)/shard_map/ppermute | solution.py:930
  19.0 2.0 %collective-permute-start.4 = (f32[2,8,128]{2,1,0:T(8,128)S(1)}, f32[2,8,128]{2,1,0:T(8,128)S(1)}, u32[]{:S(2)}, u32[]{:S(2)}) collective-permute-start(f32[2,8,128]{2,1,0:T(8,128)S(1)} %get-tuple-element.91.near), channel_id=1, source_target_pairs={{0,4},{4,0},{8,12},{12,8},{16,20},{20,16},{24,28},{28,24},{1,5},{5... | collective-permute-start | bytes 24584 | tf_op jit(solution)/shard_map/ppermute | solution.py:931
  19.1 4.0 %collective-permute-start.5 = (f32[2,8,128]{2,1,0:T(8,128)S(1)}, f32[2,8,128]{2,1,0:T(8,128)S(1)}, u32[]{:S(2)}, u32[]{:S(2)}) collective-permute-start(f32[2,8,128]{2,1,0:T(8,128)S(1)} %get-tuple-element.92.far), channel_id=1, source_target_pairs={{4,8},{8,4},{12,16},{16,12},{20,24},{24,20},{28,0},{0,28},{5,9},{9... | collective-permute-start | bytes 24584 | tf_op jit(solution)/shard_map/ppermute | solution.py:930
  23.1 3.7 %collective-permute-start.6 = (f32[2,8,128]{2,1,0:T(8,128)S(1)}, f32[2,8,128]{2,1,0:T(8,128)S(1)}, u32[]{:S(2)}, u32[]{:S(2)}) collective-permute-start(f32[2,8,128]{2,1,0:T(8,128)S(1)} %get-tuple-element.93.near), channel_id=1, source_target_pairs={{0,1},{1,0},{2,3},{3,2},{4,5},{5,4},{6,7},{7,6},{8,9},{9,8},{10,11... | collective-permute-start | bytes 24584 | tf_op jit(solution)/shard_map/ppermute | solution.py:931
  23.8 5.4 %collective-permute-start.7 = (f32[2,8,128]{2,1,0:T(8,128)S(1)}, f32[2,8,128]{2,1,0:T(8,128)S(1)}, u32[]{:S(2)}, u32[]{:S(2)}) collective-permute-start(f32[2,8,128]{2,1,0:T(8,128)S(1)} %get-tuple-element.94.far), channel_id=1, source_target_pairs={{1,2},{2,1},{3,0},{0,3},{5,6},{6,5},{7,4},{4,7},{9,10},{10,9},{11,... | collective-permute-start | bytes 24584 | tf_op jit(solution)/shard_map/ppermute | solution.py:930
  39.6 1.2 %collective-permute-start.8 = (f32[2,8,128]{2,1,0:T(8,128)S(1)}, f32[2,8,128]{2,1,0:T(8,128)S(1)}, u32[]{:S(2)}, u32[]{:S(2)}) collective-permute-start(f32[2,8,128]{2,1,0:T(8,128)S(1)} %get-tuple-element.99.near), channel_id=1, source_target_pairs={{0,4},{4,0},{8,12},{12,8},{16,20},{20,16},{24,28},{28,24},{1,5},{5... | collective-permute-start | bytes 24584 | tf_op jit(solution)/shard_map/ppermute | solution.py:931
  39.7 4.0 %collective-permute-start.9 = (f32[2,8,128]{2,1,0:T(8,128)S(1)}, f32[2,8,128]{2,1,0:T(8,128)S(1)}, u32[]{:S(2)}, u32[]{:S(2)}) collective-permute-start(f32[2,8,128]{2,1,0:T(8,128)S(1)} %get-tuple-element.100.far), channel_id=1, source_target_pairs={{4,8},{8,4},{12,16},{16,12},{20,24},{24,20},{28,0},{0,28},{5,9},{9... | collective-permute-start | bytes 24584 | tf_op jit(solution)/shard_map/ppermute | solution.py:930
  43.8 3.7 %collective-permute-start.10 = (f32[2,8,128]{2,1,0:T(8,128)S(1)}, f32[2,8,128]{2,1,0:T(8,128)S(1)}, u32[]{:S(2)}, u32[]{:S(2)}) collective-permute-start(f32[2,8,128]{2,1,0:T(8,128)S(1)} %get-tuple-element.101.near), channel_id=1, source_target_pairs={{0,1},{1,0},{2,3},{3,2},{4,5},{5,4},{6,7},{7,6},{8,9},{9,8},{10,11... | collective-permute-start | bytes 24584 | tf_op jit(solution)/shard_map/ppermute | solution.py:931
  44.3 5.4 %collective-permute-start.11 = (f32[2,8,128]{2,1,0:T(8,128)S(1)}, f32[2,8,128]{2,1,0:T(8,128)S(1)}, u32[]{:S(2)}, u32[]{:S(2)}) collective-permute-start(f32[2,8,128]{2,1,0:T(8,128)S(1)} %get-tuple-element.102.far), channel_id=1, source_target_pairs={{1,2},{2,1},{3,0},{0,3},{5,6},{6,5},{7,4},{4,7},{9,10},{10,9},{11,... | collective-permute-start | bytes 24584 | tf_op jit(solution)/shard_map/ppermute | solution.py:930
  53.9 1.6 %collective-permute-start.12 = (f32[4,128,128]{2,1,0:T(8,128)S(1)}, f32[4,128,128]{2,1,0:T(8,128)S(1)}, u32[]{:S(2)}, u32[]{:S(2)}) collective-permute-start(f32[4,128,128]{2,1,0:T(8,128)S(1)} %get-tuple-element.107), channel_id=1, source_target_pairs={{0,4},{4,0},{8,12},{12,8},{16,20},{20,16},{24,28},{28,24},{1,5},{5... | collective-permute-start | bytes 786440 | tf_op jit(solution)/shard_map/ppermute | solution.py:941
  55.5 8.4 %collective-permute-start.15 = (f32[128,128]{1,0:T(8,128)S(1)}, f32[128,128]{1,0:T(8,128)S(1)}, u32[]{:S(2)}, u32[]{:S(2)}) collective-permute-start(f32[128,128]{1,0:T(8,128)S(1)} %get-tuple-element.114), channel_id=1, source_target_pairs={{0,1},{1,0},{2,3},{3,2},{4,5},{5,4},{6,7},{7,6},{8,9},{9,8},{10,11... | collective-permute-start | bytes 196616 | tf_op jit(solution)/shard_map/ppermute | solution.py:941
  55.6 8.7 %collective-permute-start.16 = (f32[128,128]{1,0:T(8,128)S(1)}, f32[128,128]{1,0:T(8,128)S(1)}, u32[]{:S(2)}, u32[]{:S(2)}) collective-permute-start(f32[128,128]{1,0:T(8,128)S(1)} %get-tuple-element.115), channel_id=1, source_target_pairs={{0,2},{1,3},{2,0},{3,1},{4,6},{5,7},{6,4},{7,5},{8,10},{9,11},{10,... | collective-permute-start | bytes 196616 | tf_op jit(solution)/shard_map/ppermute | solution.py:941
  57.7 6.6 %collective-permute-start.17 = (f32[128,128]{1,0:T(8,128)S(1)}, f32[128,128]{1,0:T(8,128)S(1)}, u32[]{:S(2)}, u32[]{:S(2)}) collective-permute-start(f32[128,128]{1,0:T(8,128)S(1)} %get-tuple-element.116), channel_id=1, source_target_pairs={{0,3},{1,2},{2,1},{3,0},{4,7},{5,6},{6,5},{7,4},{8,11},{9,10},{10,... | collective-permute-start | bytes 196616 | tf_op jit(solution)/shard_map/ppermute | solution.py:941
  60.0 1.2 %collective-permute-start.13 = (f32[2,8,128]{2,1,0:T(8,128)S(1)}, f32[2,8,128]{2,1,0:T(8,128)S(1)}, u32[]{:S(2)}, u32[]{:S(2)}) collective-permute-start(f32[2,8,128]{2,1,0:T(8,128)S(1)} %get-tuple-element.111.near), channel_id=1, source_target_pairs={{0,4},{4,0},{8,12},{12,8},{16,20},{20,16},{24,28},{28,24},{1,5},{5... | collective-permute-start | bytes 24584 | tf_op jit(solution)/shard_map/ppermute | solution.py:931
  60.0 4.0 %collective-permute-start.14 = (f32[2,8,128]{2,1,0:T(8,128)S(1)}, f32[2,8,128]{2,1,0:T(8,128)S(1)}, u32[]{:S(2)}, u32[]{:S(2)}) collective-permute-start(f32[2,8,128]{2,1,0:T(8,128)S(1)} %get-tuple-element.112.far), channel_id=1, source_target_pairs={{4,8},{8,4},{12,16},{16,12},{20,24},{24,20},{28,0},{0,28},{5,9},{9... | collective-permute-start | bytes 24584 | tf_op jit(solution)/shard_map/ppermute | solution.py:930
  64.3 10.3 %collective-permute-start.22 = (f32[128,128]{1,0:T(8,128)S(1)}, f32[128,128]{1,0:T(8,128)S(1)}, u32[]{:S(2)}, u32[]{:S(2)}) collective-permute-start(f32[128,128]{1,0:T(8,128)S(1)} %get-tuple-element.119.refs_0_), channel_id=1, source_target_pairs={{0,24},{4,28},{8,16},{12,20},{16,8},{20,12},{24,0},{28,4},{1,25},{... | collective-permute-start | bytes 196616 | tf_op jit(solution)/shard_map/ppermute | solution.py:941
  64.4 10.2 %collective-permute-start.21 = (f32[128,128]{1,0:T(8,128)S(1)}, f32[128,128]{1,0:T(8,128)S(1)}, u32[]{:S(2)}, u32[]{:S(2)}) collective-permute-start(f32[128,128]{1,0:T(8,128)S(1)} %get-tuple-element.119.refs_0_), channel_id=1, source_target_pairs={{0,16},{4,20},{8,24},{12,28},{16,0},{20,4},{24,8},{28,12},{1,17},{... | collective-permute-start | bytes 196616 | tf_op jit(solution)/shard_map/ppermute | solution.py:941
  65.5 9.1 %collective-permute-start.20 = (f32[128,128]{1,0:T(8,128)S(1)}, f32[128,128]{1,0:T(8,128)S(1)}, u32[]{:S(2)}, u32[]{:S(2)}) collective-permute-start(f32[128,128]{1,0:T(8,128)S(1)} %get-tuple-element.119.refs_0_), channel_id=1, source_target_pairs={{0,8},{4,12},{8,0},{12,4},{16,24},{20,28},{24,16},{28,20},{1,9},{5... | collective-permute-start | bytes 196616 | tf_op jit(solution)/shard_map/ppermute | solution.py:941
  67.9 3.7 %collective-permute-start.18 = (f32[2,8,128]{2,1,0:T(8,128)S(1)}, f32[2,8,128]{2,1,0:T(8,128)S(1)}, u32[]{:S(2)}, u32[]{:S(2)}) collective-permute-start(f32[2,8,128]{2,1,0:T(8,128)S(1)} %get-tuple-element.117.near), channel_id=1, source_target_pairs={{0,1},{1,0},{2,3},{3,2},{4,5},{5,4},{6,7},{7,6},{8,9},{9,8},{10,11... | collective-permute-start | bytes 24584 | tf_op jit(solution)/shard_map/ppermute | solution.py:931
  69.1 5.4 %collective-permute-start.19 = (f32[2,8,128]{2,1,0:T(8,128)S(1)}, f32[2,8,128]{2,1,0:T(8,128)S(1)}, u32[]{:S(2)}, u32[]{:S(2)}) collective-permute-start(f32[2,8,128]{2,1,0:T(8,128)S(1)} %get-tuple-element.118.far), channel_id=1, source_target_pairs={{1,2},{2,1},{3,0},{0,3},{5,6},{6,5},{7,4},{4,7},{9,10},{10,9},{11,... | collective-permute-start | bytes 24584 | tf_op jit(solution)/shard_map/ppermute | solution.py:930
  74.6 1.3 %collective-permute-start.23 = (f32[128,128]{1,0:T(8,128)S(1)}, f32[128,128]{1,0:T(8,128)S(1)}, u32[]{:S(2)}, u32[]{:S(2)}) collective-permute-start(f32[128,128]{1,0:T(8,128)S(1)} %get-tuple-element.120.mine), channel_id=1, source_target_pairs={{0,4},{4,0},{8,12},{12,8},{16,20},{20,16},{24,28},{28,24},{1,5},{5... | collective-permute-start | bytes 196616 | tf_op jit(solution)/shard_map/ppermute | solution.py:941
